TPU v7x, 32 devices: a whole 2x2x4 slice. The times are simulated.
32 devices in a mesh: dp: 4 (over y, x), expert: 8 (over z, core).
Axes of the slice: x: 2, y: 2, z: 4, core: 2. Of those that a mesh axis runs over, the one named last changes fastest.
Arguments:
- tokens: bfloat16 [1024, 1024], P(('dp', 'expert')), may hold values from -6 to 6
- cotangent: bfloat16 [1024, 1024], P(('dp', 'expert')), may hold values from -3 to 3
- routes: int32 [1024, 8], P(('dp', 'expert')), may hold values from 0 to 7, as said below
- combine: bfloat16 [1024, 8], P(('dp', 'expert')), may hold values from 0.099609375 to 1
- hot_experts: int32 [4], replicated, may hold values from 0 to 3, as said below
- extra_slots: int32 [4], replicated, may hold values from 1 to 4, as said below
- w_gate: bfloat16 [8, 1024, 384], P('expert'), may hold values from -0.1875 to 0.1875
- w_up: bfloat16 [8, 1024, 384], P('expert'), may hold values from -0.1875 to 0.1875
- w_down: bfloat16 [8, 384, 1024], P('expert'), may hold values from -0.3125 to 0.3125
Outputs:
- token_grads: bfloat16 [1024, 1024], P(('dp', 'expert'))
- grad_gate: bfloat16 [8, 1024, 384], P('expert', 'dp')
- grad_up: bfloat16 [8, 1024, 384], P('expert', 'dp')
- grad_down: bfloat16 [8, 384, 1024], P('expert')
Inputs may be any that keep to these rules, and one draw needn't show every extreme that they name: `routes`: each row names 8 different experts. `hot_experts`: 4 different experts, all below 4. `extra_slots`: one of the entries equals 4.
All inputs are finite; a program needn't handle non-finite values.
Results may differ from a plain program's by a relative error of at most 0.0064.
Values may be sent and summed in bfloat16 or wider, within the bound.
A program may use at most 64 MiB of HBM per device.

v0:
```python
import functools

import jax
import jax.numpy as jnp
from jax import lax
from jax.experimental import pallas as pl
from jax.experimental.pallas import tpu as pltpu
from jax.sharding import PartitionSpec as P


def forward_rows(weight_gate, weight_up, weight_down, row_tokens, row_cotan, row_weights):
    gate_pre = jnp.dot(row_tokens, weight_gate, preferred_element_type=jnp.float32)
    up_proj = jnp.dot(row_tokens, weight_up, preferred_element_type=jnp.float32)
    sigmoid_gate = jax.nn.sigmoid(gate_pre)
    gate_act = gate_pre * sigmoid_gate
    hidden = (gate_act * up_proj).astype(jnp.bfloat16)
    out_grad = (row_weights.astype(jnp.float32)[:, None] * row_cotan.astype(jnp.float32)).astype(
        jnp.bfloat16
    )
    hidden_grad = jnp.dot(out_grad, weight_down.T, preferred_element_type=jnp.float32)
    gate_grad = (
        hidden_grad * up_proj * sigmoid_gate * (1.0 + gate_pre * (1.0 - sigmoid_gate))
    ).astype(jnp.bfloat16)
    up_grad = (hidden_grad * gate_act).astype(jnp.bfloat16)
    row_grads = jnp.dot(gate_grad, weight_gate.T, preferred_element_type=jnp.float32)
    row_grads = row_grads + jnp.dot(up_grad, weight_up.T, preferred_element_type=jnp.float32)
    return (row_grads.astype(jnp.bfloat16), (row_tokens, gate_grad, up_grad, hidden, out_grad))


def weight_terms(pieces):
    row_tokens, gate_grad, up_grad, hidden, out_grad = pieces
    grad_gate = jnp.dot(row_tokens.T, gate_grad, preferred_element_type=jnp.float32)
    grad_up = jnp.dot(row_tokens.T, up_grad, preferred_element_type=jnp.float32)
    grad_down = jnp.dot(hidden.T, out_grad, preferred_element_type=jnp.float32)
    return (grad_gate, grad_up, grad_down)


def expert_pass(weight_gate, weight_up, weight_down, row_tokens, row_cotan, row_weights):
    row_grads, pieces = forward_rows(
        weight_gate, weight_up, weight_down, row_tokens, row_cotan, row_weights
    )
    return (row_grads, weight_terms(pieces))


def shards(tokens, cotangent, routes, combine, hot_experts, extra_slots, w_gate, w_up, w_down):
    expert_count = lax.axis_size("expert")
    token_count, features = tokens.shape
    route_count = routes.shape[1]
    capacity = max(2, min(token_count * route_count * 7 // (8 * expert_count), token_count // 2))
    spare_slots = 2 * max(1, capacity // 6)
    expert_ids = routes.reshape(-1)
    assign_count = expert_ids.shape[0]
    assign_order = jnp.arange(assign_count, dtype=jnp.int32)
    earlier = (expert_ids[:, None] == expert_ids[None, :]) & (
        assign_order[None, :] < assign_order[:, None]
    )
    slot_rank = jnp.sum(earlier.astype(jnp.int32), axis=1)
    hot_match = expert_ids[:, None] == hot_experts[None, :]
    slot_limit = capacity + jnp.sum(jnp.where(hot_match, extra_slots[None, :], 0), axis=1)
    is_kept = slot_rank < slot_limit
    slot_count = capacity + spare_slots
    total_slots = expert_count * slot_count
    flat_slot = jnp.where(is_kept, expert_ids * slot_count + slot_rank, total_slots)
    slot_ids = jnp.arange(total_slots, dtype=jnp.int32)
    assign_onehot = slot_ids[:, None] == flat_slot[None, :]
    token_onehot = jnp.any(
        assign_onehot.reshape(total_slots, token_count, route_count), axis=2
    ).astype(jnp.bfloat16)
    both_rows = jnp.concatenate([tokens, cotangent], axis=1)
    filled = jnp.dot(token_onehot, both_rows, preferred_element_type=jnp.float32).astype(
        jnp.bfloat16
    )
    token_send = filled[:, :features].reshape(expert_count, slot_count, features)
    cotan_send = filled[:, features:].reshape(expert_count, slot_count, features)
    weight_flat = jnp.sum(
        jnp.where(assign_onehot, combine.reshape(-1).astype(jnp.float32)[None, :], 0.0), axis=1
    )
    weight_send = weight_flat.astype(jnp.bfloat16).reshape(expert_count, slot_count)
    token_recv, cotan_recv, weight_recv = (
        lax.all_to_all(token_send, "expert", split_axis=0, concat_axis=0, tiled=True),
        lax.all_to_all(cotan_send, "expert", split_axis=0, concat_axis=0, tiled=True),
        lax.all_to_all(weight_send, "expert", split_axis=0, concat_axis=0, tiled=True),
    )
    own_weights = (w_gate[0], w_up[0], w_down[0])
    all_rows, grad_terms = expert_pass(
        own_weights[0],
        own_weights[1],
        own_weights[2],
        token_recv.reshape(-1, features),
        cotan_recv.reshape(-1, features),
        weight_recv.reshape(-1),
    )
    grad_rows = all_rows.reshape(expert_count, slot_count, features)
    returned_rows = lax.all_to_all(grad_rows, "expert", split_axis=0, concat_axis=0, tiled=True)
    token_grads = jnp.dot(
        token_onehot.T,
        returned_rows.reshape(total_slots, features),
        preferred_element_type=jnp.float32,
    ).astype(jnp.bfloat16)
    grad_gate, grad_up = (
        lax.psum_scatter(grad_terms[0][None], "dp", scatter_dimension=1, tiled=True),
        lax.psum_scatter(grad_terms[1][None], "dp", scatter_dimension=1, tiled=True),
    )
    grad_down = lax.psum(grad_terms[2][None], "dp")
    return (
        token_grads,
        grad_gate.astype(jnp.bfloat16),
        grad_up.astype(jnp.bfloat16),
        grad_down.astype(jnp.bfloat16),
    )


MESH = pl.DeviceIdType.MESH
LANES = 128
TILE = 16
NT = (((1,), (1,)), ((), ()))
TN = (((0,), (0,)), ((), ()))


def slots_of(token_count, route_count, expert_count):
    capacity = max(2, min(token_count * route_count * 7 // (8 * expert_count), token_count // 2))
    return capacity, 2 * max(1, capacity // 6)


def dense_fits(sizes, token_count, features, route_count, hidden_size):
    capacity, spare = slots_of(token_count, route_count, sizes["expert"])
    return (
        route_count == sizes["expert"]
        and sizes["dp"] == 4
        and sizes["expert"] % 2 == 0
        and token_count == 2 * TILE
        and capacity == TILE
        and spare * 2 == 8
        and features % (8 * LANES) == 0
        and hidden_size % LANES == 0
    )


def dense_kernel(
    experts,
    tok_hbm,
    cot_hbm,
    routes_hbm,
    comb_hbm,
    hot_hbm,
    extra_hbm,
    wg_hbm,
    wu_hbm,
    wd_hbm,
    tg_ref,
    gg_out,
    gu_out,
    gd_out,
    tok_ref,
    cot_ref,
    routes_ref,
    comb_ref,
    hot_ref,
    extra_ref,
    in_sem,
    slab,
    wg,
    wu,
    wd,
    all_t,
    all_og,
    all_h,
    all_gg,
    all_ug,
    acc_gate,
    acc_up,
    acc_down,
    row_out,
    pair_in,
    pair_sum,
    z_in,
    w_sem,
    send_sem,
    recv_sem,
    pair_send,
    pair_recv,
    z_send,
    z_recv,
):
    levels = experts // 2
    features = tok_ref.shape[1]
    blocks = features // LANES
    half = blocks // 2
    spill_at = 2 * blocks
    weight_at = spill_at + half
    bf16, f32 = jnp.bfloat16, jnp.float32

    d = lax.axis_index("dp")
    e = lax.axis_index("expert")
    z, c = e // 2, e % 2
    dx = d + 1 - 2 * (d % 2)
    dy = (d + 2) % 4
    dd = 3 - d
    pc = 1 - c

    def to(dp, level, core):
        return (dp, level * 2 + core)

    def slab_id(dp, level, core):
        return dp * experts + level * 2 + core

    input_copies = [
        pltpu.make_async_copy(h, v, in_sem.at[i])
        for i, (h, v) in enumerate(
            (
                (tok_hbm, tok_ref),
                (cot_hbm, cot_ref),
                (routes_hbm, routes_ref),
                (comb_hbm, comb_ref),
                (hot_hbm, hot_ref),
                (extra_hbm, extra_ref),
            )
        )
    ]
    for copy in input_copies:
        copy.start()
    weight_copies = [
        pltpu.make_async_copy(h.at[0], v, w_sem.at[i])
        for i, (h, v) in enumerate(((wg_hbm, wg), (wu_hbm, wu), (wd_hbm, wd)))
    ]
    for copy in weight_copies:
        copy.start()

    barrier = pltpu.get_barrier_semaphore()
    for peer in (to(dx, z, c), to(dy, z, c), to(d, z, pc)):
        pl.semaphore_signal(barrier, inc=1, device_id=peer, device_id_type=MESH)
    for step in range(1, levels):
        pl.semaphore_signal(
            barrier, inc=1, device_id=to(d, (z + step) % levels, c), device_id_type=MESH
        )

    me = slab_id(d, z, c)
    for copy in input_copies:
        copy.wait()
    names = -(-experts // TILE) * TILE
    expert_row = lax.broadcasted_iota(jnp.int32, (names, 2 * TILE), 0)
    token_lane = lax.broadcasted_iota(jnp.int32, (names, 2 * TILE), 1)
    routes = routes_ref[...]
    comb = comb_ref[...].astype(f32)
    weights = jnp.zeros((names, 2 * TILE), f32)
    for r in range(routes.shape[0]):
        weights = jnp.where(expert_row == routes[r : r + 1, :], comb[r : r + 1, :], weights)
    limit = jnp.full((names, 2 * TILE), TILE, jnp.int32)
    for j in range(hot_ref.shape[0]):
        limit = limit + jnp.where(expert_row == hot_ref[j], extra_ref[j], 0)
    weights = jnp.where(token_lane < limit, weights, 0.0).astype(bf16)
    unit_row = lax.broadcasted_iota(jnp.int32, (names, LANES), 0)
    unit_lane = lax.broadcasted_iota(jnp.int32, (names, LANES), 1)

    def turned(shift):
        unit = jnp.where(unit_lane == unit_row + shift, 1.0, 0.0).astype(bf16)
        return lax.dot_general(weights, unit, TN, preferred_element_type=f32)

    main_part, tail_part = turned(0), turned(LANES // 2)
    slab[me, weight_at] = (main_part[:TILE] + tail_part[TILE:]).astype(bf16)
    tok_tail = tok_ref[TILE:, :].astype(f32)[:8]
    cot_tail = cot_ref[TILE:, :].astype(f32)[:8]
    tail_row = lax.broadcasted_iota(jnp.int32, (8, features), 0)
    spill = jnp.where(tail_row < 4, tok_tail, pltpu.roll(cot_tail, 4, 0))
    for j in range(blocks):
        cols = slice(j * LANES, (j + 1) * LANES)
        slab[me, j] = tok_ref[:TILE, cols]
        slab[me, blocks + j] = cot_ref[:TILE, cols]
    for j in range(half):
        lo = spill[:, j * LANES : (j + 1) * LANES]
        hi = spill[:, (half + j) * LANES : (half + j + 1) * LANES]
        slab[me, spill_at + j] = jnp.concatenate([lo, hi], axis=0).astype(bf16)

    pl.semaphore_wait(barrier, 3 + levels - 1)

    tiles = slab.shape[1]
    cut = (tiles + 1) // 2
    pieces = (pl.ds(0, cut), pl.ds(cut, tiles - cut))

    def copy_of(s, p, way, peer):
        return pltpu.make_async_remote_copy(
            src_ref=slab.at[s, pieces[p]],
            dst_ref=slab.at[s, pieces[p]],
            send_sem=send_sem.at[way, p, s],
            recv_sem=recv_sem.at[p, s],
            device_id=peer,
            device_id_type=MESH,
        )

    def to_x(s, p):
        return copy_of(s, p, 0, to(dx, z, c))

    def to_y(s, p):
        return copy_of(s, p, 1, to(dy, z, c))

    def to_pair(s, p):
        return copy_of(s, p, 2, to(d, z, pc))

    def to_level(p, step):
        return copy_of(me, p, 2 + step, to(d, (z + step) % levels, c))

    def arrived(s, p):
        to_pair(s, p).wait_recv()

    def at_distance(dist, visit):
        if dist == 0:
            visit(z, 0)
            return
        pl.when(z - dist >= 0)(lambda: visit(z - dist, -1))
        pl.when(z + dist < levels)(lambda: visit(z + dist, 1))

    def column(dist, p):
        def visit(level, side):
            s = slab_id(d, level, c)
            if side:
                arrived(s, p)
            to_x(s, p).start()
            to_y(s, p).start()
            if side == 0:
                for step in range(1, levels):
                    to_level(p, step).start()
            to_pair(s, p).start()

        at_distance(dist, visit)

    def beside(dist, p):
        def visit(level, side):
            for dp in (dx, dy):
                s = slab_id(dp, level, c)
                arrived(s, p)
                if p == 0 and dp is dx:
                    to_y(s, p).start()
                if p == 1 and dp is dy:
                    to_x(s, p).start()
                to_pair(s, p).start()

        at_distance(dist, visit)

    def across(dist):
        def visit(level, side):
            s = slab_id(dd, level, c)
            for p in (0, 1):
                arrived(s, p)
                to_pair(s, p).start()

        at_distance(dist, visit)

    def from_pair(dp):
        for level in range(levels):
            for p in (0, 1):
                arrived(slab_id(dp, level, pc), p)

    column(0, 0)
    column(0, 1)
    for dist in range(1, levels):
        for p in (0, 1):
            column(dist, p)
    from_pair(d)

    main_rows = experts * TILE
    group_rows = main_rows + experts * 8
    main_lane = lax.broadcasted_iota(jnp.int32, (main_rows, LANES), 1)
    tail_lane = lax.broadcasted_iota(jnp.int32, (experts * 8, LANES), 1)

    def group(dp, at):
        rows = pl.ds(at, group_rows)
        part = pl.ds(dp * experts, experts)

        def main(j):
            return slab[part, j].reshape(main_rows, LANES)

        lo, hi = [], []
        for j in range(half):
            both = slab[part, spill_at + j].astype(f32)
            lo.append(both[:, :8].reshape(experts * 8, LANES))
            hi.append(both[:, 8:].reshape(experts * 8, LANES))
        tail = jnp.concatenate(lo + hi, axis=1)
        cot_rows = pltpu.roll(tail, experts * 8 - 4, 0)
        w_all = slab[part, weight_at].astype(f32)
        w_main = w_all.reshape(main_rows, LANES)
        w_tail = w_all[:, :8].reshape(experts * 8, LANES)
        w = jnp.concatenate(
            [
                jnp.sum(jnp.where(main_lane == e, w_main, 0.0), axis=1, keepdims=True),
                jnp.sum(jnp.where(tail_lane == e + LANES // 2, w_tail, 0.0), axis=1, keepdims=True),
            ],
            axis=0,
        )
        all_t[rows, :] = jnp.concatenate(
            [jnp.concatenate([main(j) for j in range(blocks)], axis=1), tail.astype(bf16)], axis=0
        )
        cot = jnp.concatenate(
            [
                jnp.concatenate([main(blocks + j) for j in range(blocks)], axis=1).astype(f32),
                cot_rows,
            ],
            axis=0,
        )
        all_og[rows, :] = (w * cot).astype(bf16)
        t = all_t[rows, :]
        gate_pre = jnp.dot(t, wg[...], preferred_element_type=f32)
        up_proj = jnp.dot(t, wu[...], preferred_element_type=f32)
        hidden_grad = lax.dot_general(all_og[rows, :], wd[...], NT, preferred_element_type=f32)
        sig = jax.nn.sigmoid(gate_pre)
        act = gate_pre * sig
        all_h[rows, :] = (act * up_proj).astype(bf16)
        all_gg[rows, :] = (hidden_grad * up_proj * sig * (1.0 + gate_pre * (1.0 - sig))).astype(
            bf16
        )
        all_ug[rows, :] = (hidden_grad * act).astype(bf16)

    for copy in weight_copies:
        copy.wait()
    group(d, 0)
    own = pl.ds(0, group_rows)
    rg = lax.dot_general(all_gg[own, :], wg[...], NT, preferred_element_type=f32)
    rg = rg + lax.dot_general(all_ug[own, :], wu[...], NT, preferred_element_type=f32)
    for j in range(blocks):
        row_out[:, j] = (
            rg[:main_rows, j * LANES : (j + 1) * LANES].reshape(experts, TILE, LANES).astype(bf16)
        )
    for j in range(half):
        lo = rg[main_rows:, j * LANES : (j + 1) * LANES].reshape(experts, 8, LANES)
        hi = rg[main_rows:, (half + j) * LANES : (half + j + 1) * LANES].reshape(experts, 8, LANES)
        row_out[:, blocks + j] = jnp.concatenate([lo, hi], axis=1).astype(bf16)

    def pair_copy(level):
        return pltpu.make_async_remote_copy(
            src_ref=row_out.at[level * 2 + pc],
            dst_ref=pair_in.at[level],
            send_sem=pair_send.at[level],
            recv_sem=pair_recv.at[level],
            device_id=to(d, z, pc),
            device_id_type=MESH,
        )

    for level in range(levels):
        pair_copy(level).start()

    for dist in range(levels):
        for p in (0, 1):
            beside(dist, p)

    for level in range(levels):
        pair_copy(level).wait_recv()
        pair_sum[level] = (
            row_out[level * 2 + c].astype(f32) + pair_in[level].astype(f32)
        ).astype(bf16)

    def z_copy(step):
        level = (z + step) % levels
        return pltpu.make_async_remote_copy(
            src_ref=pair_sum.at[level],
            dst_ref=z_in.at[step - 1],
            send_sem=z_send.at[step - 1],
            recv_sem=z_recv.at[step - 1],
            device_id=to(d, level, c),
            device_id_type=MESH,
        )

    for step in range(1, levels):
        z_copy(step).start()

    from_pair(dx)
    group(dx, group_rows)
    from_pair(dy)
    group(dy, 2 * group_rows)
    for dist in range(levels):
        across(dist)
    share = features // 4

    def weight_terms(at, count):
        rows = pl.ds(at, count)
        t_cols = all_t[rows, pl.ds(pl.multiple_of(d * share, LANES), share)]
        return (
            lax.dot_general(t_cols, all_gg[rows, :], TN, preferred_element_type=f32),
            lax.dot_general(t_cols, all_ug[rows, :], TN, preferred_element_type=f32),
            lax.dot_general(all_h[rows, :], all_og[rows, :], TN, preferred_element_type=f32),
        )

    early = weight_terms(0, 3 * group_rows)
    acc_gate[...], acc_up[...], acc_down[...] = early
    from_pair(dd)
    group(dd, 3 * group_rows)
    late = weight_terms(3 * group_rows, group_rows)
    gg_out[0] = (acc_gate[...] + late[0]).astype(bf16)
    gu_out[0] = (acc_up[...] + late[1]).astype(bf16)
    gd_out[0] = (acc_down[...] + late[2]).astype(bf16)

    total = pair_sum[z].astype(f32)
    for step in range(1, levels):
        z_copy(step).wait_recv()
        total = total + z_in[step - 1].astype(f32)
    for j in range(blocks):
        tg_ref[:TILE, j * LANES : (j + 1) * LANES] = total[j].astype(bf16)
    blank = jnp.zeros((8, LANES), f32)
    for j in range(half):
        tile = total[blocks + j]
        tg_ref[TILE:, j * LANES : (j + 1) * LANES] = jnp.concatenate(
            [tile[:8], blank], axis=0
        ).astype(bf16)
        tg_ref[TILE:, (half + j) * LANES : (half + j + 1) * LANES] = jnp.concatenate(
            [tile[8:], blank], axis=0
        ).astype(bf16)

    for level in range(levels):
        pair_copy(level).wait_send()
        to_y(slab_id(dx, level, c), 0).wait_send()
        to_x(slab_id(dy, level, c), 1).wait_send()
        s = slab_id(d, level, c)
        for p in (0, 1):
            to_x(s, p).wait_send()
            to_y(s, p).wait_send()
            for dp in (d, dx, dy, dd):
                to_pair(slab_id(dp, level, c), p).wait_send()

    for step in range(1, levels):
        z_copy(step).wait_send()
        to_level(0, step).wait_send()
        to_level(1, step).wait_send()


def write_kernel(*refs):
    sources, sem = refs[: len(refs) // 2], refs[-1]
    targets = refs[len(refs) // 2 : -1]
    copies = [
        pltpu.make_async_copy(a, b, sem.at[i]) for i, (a, b) in enumerate(zip(sources, targets))
    ]
    for copy in copies:
        copy.start()
    for copy in copies:
        copy.wait()


def dense_shards(tokens, cotangent, routes, combine, hot_experts, extra_slots, w_gate, w_up, w_down):
    experts = lax.axis_size("expert")
    replicas = lax.axis_size("dp")
    token_count, features = tokens.shape
    hidden_size = w_gate.shape[2]
    blocks = features // LANES
    levels = experts // 2
    tiles = 2 * blocks + blocks // 2 + 1
    back = blocks + blocks // 2
    rows = replicas * experts * (TILE + 8)
    bf16 = jnp.bfloat16
    vmem = pl.BlockSpec(memory_space=pltpu.VMEM)
    hbm = pl.BlockSpec(memory_space=pltpu.HBM)
    dma = pltpu.SemaphoreType.DMA
    operands = [
        pltpu.with_memory_space_constraint(a, pltpu.HBM)
        for a in (
            tokens,
            cotangent,
            routes.T,
            combine.T,
            hot_experts,
            extra_slots,
            w_gate,
            w_up,
            w_down,
        )
    ]
    results = pl.pallas_call(
        functools.partial(dense_kernel, experts),
        out_shape=(
            jax.ShapeDtypeStruct((token_count, features), bf16),
            jax.ShapeDtypeStruct((1, features // replicas, hidden_size), bf16),
            jax.ShapeDtypeStruct((1, features // replicas, hidden_size), bf16),
            jax.ShapeDtypeStruct((1, hidden_size, features), bf16),
        ),
        in_specs=[hbm] * 9,
        out_specs=(vmem, vmem, vmem, vmem),
        scratch_shapes=[
            pltpu.VMEM(tokens.shape, bf16),
            pltpu.VMEM(tokens.shape, bf16),
            pltpu.VMEM(routes.shape[::-1], jnp.int32),
            pltpu.VMEM(routes.shape[::-1], bf16),
            pltpu.SMEM(hot_experts.shape, jnp.int32),
            pltpu.SMEM(hot_experts.shape, jnp.int32),
            dma((6,)),
            pltpu.VMEM((replicas * experts, tiles, TILE, LANES), bf16),
            pltpu.VMEM((features, hidden_size), bf16),
            pltpu.VMEM((features, hidden_size), bf16),
            pltpu.VMEM((hidden_size, features), bf16),
            pltpu.VMEM((rows, features), bf16),
            pltpu.VMEM((rows, features), bf16),
            pltpu.VMEM((rows, hidden_size), bf16),
            pltpu.VMEM((rows, hidden_size), bf16),
            pltpu.VMEM((rows, hidden_size), bf16),
            pltpu.VMEM((features // replicas, hidden_size), jnp.float32),
            pltpu.VMEM((features // replicas, hidden_size), jnp.float32),
            pltpu.VMEM((hidden_size, features), jnp.float32),
            pltpu.VMEM((experts, back, TILE, LANES), bf16),
            pltpu.VMEM((levels, back, TILE, LANES), bf16),
            pltpu.VMEM((levels, back, TILE, LANES), bf16),
            pltpu.VMEM((levels - 1, back, TILE, LANES), bf16),
            dma((3,)),
            dma((levels + 2, 2, replicas * experts)),
            dma((2, replicas * experts)),
            dma((levels,)),
            dma((levels,)),
            dma((levels - 1,)),
            dma((levels - 1,)),
        ],
        compiler_params=pltpu.CompilerParams(
            collective_id=0, has_side_effects=True, vmem_limit_bytes=32 * 1024 * 1024
        ),
    )(*operands)
    return pl.pallas_call(
        write_kernel,
        out_shape=tuple(jax.ShapeDtypeStruct(r.shape, r.dtype) for r in results),
        in_specs=[vmem] * len(results),
        out_specs=tuple(hbm for _ in results),
        scratch_shapes=[dma((len(results),))],
        compiler_params=pltpu.CompilerParams(vmem_limit_bytes=8 * 1024 * 1024),
    )(*results)


def solution(mesh):
    in_specs = (
        P(("dp", "expert"), None),
        P(("dp", "expert"), None),
        P(("dp", "expert"), None),
        P(("dp", "expert"), None),
        P(),
        P(),
        P("expert", None, None),
        P("expert", None, None),
        P("expert", None, None),
    )
    out_specs = (
        P(("dp", "expert"), None),
        P("expert", "dp", None),
        P("expert", "dp", None),
        P("expert", None, None),
    )

    def body(*args):
        token_count, features = args[0].shape
        if dense_fits(dict(mesh.shape), token_count, features, args[2].shape[1], args[6].shape[2]):
            return dense_shards(*args)
        return shards(*args)

    return jax.shard_map(body, mesh=mesh, in_specs=in_specs, out_specs=out_specs, check_vma=False)
```

profile of v0, /device:TPU:0, one launch (start us, length us, event | category | flops | bytes accessed | tf_op | source)
XLA Modules:
  0.0 29.9 jit_solution(2395813359847272964)
XLA Ops:
  0.6 28.2 %shard_map.120 = (bf16[32,1024]{1,0:T(8,128)(2,1)S(1)}, bf16[1,256,384]{2,1,0:T(8,128)(2,1)S(1)}, bf16[1,256,384]{2,1,0:T(8,128)(2,1)S(1)}, bf16[1,384,1024]{2,1,0:T(8,128)(2,1)S(1)}) custom-call(bf16[32,1024]{1,0:T(8,128)(2,1)} %tok_hbm.1, bf16[32,1024]{1,0:T(8,128)(2,1)} %cot_hbm.1, s32[8,32]{1,0:T(8,128)} %bitcast.2, bf16[8,32]{1,0:T(8,128)(2,1)} %bitcast.3, ...), custom_call_target="tpu_custom_call" | custom-call | tf_op jit(solution)/shard_map/pallas_call | solution.py:563
  28.9 1.1 %shard_map.121 = (bf16[32,1024]{1,0:T(8,128)(2,1)}, bf16[1,256,384]{2,1,0:T(8,128)(2,1)}, bf16[1,256,384]{2,1,0:T(8,128)(2,1)}, bf16[1,384,1024]{2,1,0:T(8,128)(2,1)}) custom-call(bf16[32,1024]{1,0:T(8,128)(2,1)S(1)} %get-tuple-element.8.refs_0_, bf16[1,256,384]{2,1,0:T(8,128)(2,1)S(1)} %get-tuple-element.9.refs_1_, ...), custom_call_target="tpu_custom_call" | custom-call | tf_op jit(solution)/shard_map/pallas_call | solution.py:609
where the time goes:
time: 30.1 us; the launch traced here: 29.9 us
  Pallas kernels  29.3 us (97%)
  between operations  0.64 us (2%)
    pallas_call x1, Pallas kernels, dense_shards(): pl.pallas_call(functools.partial(dense_kernel, experts), out_shape=(jax.S...  28.2 us
    pallas_call x1, Pallas kernels, dense_shards(): pl.pallas_call(write_kernel, out_shape=tuple((jax.ShapeDtypeStruct(r.shap...  1.07 us

commit v1 on v0

--- a/solution.py
+++ b/solution.py
@@ -127,7 +127,7 @@
     return (
         route_count == sizes["expert"]
         and sizes["dp"] == 4
-        and sizes["expert"] % 2 == 0
+        and sizes["expert"] % 4 == 0
         and token_count == 2 * TILE
         and capacity == TILE
         and spare * 2 == 8
@@ -158,7 +158,9 @@
     hot_ref,
     extra_ref,
     in_sem,
-    slab,
+    all_tok,
+    all_cot,
+    small,
     wg,
     wu,
     wd,
@@ -170,24 +172,29 @@
     acc_gate,
     acc_up,
     acc_down,
-    row_out,
-    pair_in,
-    pair_sum,
-    z_in,
+    row_main,
+    row_tail,
+    pair_main,
+    pair_tail,
+    sum_main,
+    sum_tail,
+    z_main,
+    z_tail,
     w_sem,
+    own_sem,
     send_sem,
     recv_sem,
     pair_send,
     pair_recv,
     z_send,
     z_recv,
+    ready,
 ):
     levels = experts // 2
-    features = tok_ref.shape[1]
+    hot_levels = levels // 2
+    features = all_tok.shape[2]
     blocks = features // LANES
     half = blocks // 2
-    spill_at = 2 * blocks
-    weight_at = spill_at + half
     bf16, f32 = jnp.bfloat16, jnp.float32
 
     d = lax.axis_index("dp")
@@ -197,19 +204,23 @@
     dy = (d + 2) % 4
     dd = 3 - d
     pc = 1 - c
-
-    def to(dp, level, core):
-        return (dp, level * 2 + core)
+    hot = z < hot_levels
+    low_x, low_y, low_z = d % 2 == 1, d // 2 == 1, z > 0
+    up_x, up_y, up_z = d % 2 == 0, d // 2 == 0, z < levels - 1
+    at_x, at_y, at_pair = (dx, e), (dy, e), (d, z * 2 + pc)
+    at_down, at_up = (d, jnp.maximum(e - 2, 0)), (d, jnp.minimum(e + 2, experts - 1))
 
     def slab_id(dp, level, core):
         return dp * experts + level * 2 + core
 
+    me = slab_id(d, z, c)
+    tail_rows = pl.ds(TILE, TILE)
     input_copies = [
         pltpu.make_async_copy(h, v, in_sem.at[i])
         for i, (h, v) in enumerate(
             (
-                (tok_hbm, tok_ref),
-                (cot_hbm, cot_ref),
+                (tok_hbm.at[tail_rows], tok_ref),
+                (cot_hbm.at[tail_rows], cot_ref),
                 (routes_hbm, routes_ref),
                 (comb_hbm, comb_ref),
                 (hot_hbm, hot_ref),
@@ -217,24 +228,94 @@
             )
         )
     ]
-    for copy in input_copies:
-        copy.start()
+    own_copies = [
+        pltpu.make_async_copy(h.at[pl.ds(0, TILE)], v.at[me], own_sem.at[i])
+        for i, (h, v) in enumerate(((tok_hbm, all_tok), (cot_hbm, all_cot)))
+    ]
     weight_copies = [
         pltpu.make_async_copy(h.at[0], v, w_sem.at[i])
         for i, (h, v) in enumerate(((wg_hbm, wg), (wu_hbm, wu), (wd_hbm, wd)))
     ]
-    for copy in weight_copies:
+
+    barrier = pltpu.get_barrier_semaphore()
+
+    def greet(peer):
+        pl.semaphore_signal(barrier, inc=1, device_id=peer, device_id_type=MESH)
+
+    greet(at_pair)
+    pl.when(up_x)(lambda: greet(at_x))
+    pl.when(up_y)(lambda: greet(at_y))
+    pl.when(up_z)(lambda: greet(at_up))
+    for copy in input_copies + own_copies + weight_copies:
         copy.start()
 
-    barrier = pltpu.get_barrier_semaphore()
-    for peer in (to(dx, z, c), to(dy, z, c), to(d, z, pc)):
-        pl.semaphore_signal(barrier, inc=1, device_id=peer, device_id_type=MESH)
-    for step in range(1, levels):
-        pl.semaphore_signal(
-            barrier, inc=1, device_id=to(d, (z + step) % levels, c), device_id_type=MESH
-        )
-
-    me = slab_id(d, z, c)
+    def piece(s, p, full):
+        if p == 0:
+            return all_tok.at[s]
+        if p == 1:
+            return all_cot.at[s]
+        return small.at[s] if full else small.at[s, pl.ds(half, 1)]
+
+    def copy_of(s, p, full, way, peer, own=False):
+        dst = piece(s, p, full)
+        src = dst
+        if own and p < 2:
+            src = (tok_hbm, cot_hbm)[p].at[pl.ds(0, TILE)]
+        return pltpu.make_async_remote_copy(
+            src_ref=src,
+            dst_ref=dst,
+            send_sem=send_sem.at[way, p, s],
+            recv_sem=recv_sem.at[p, s],
+            device_id=peer,
+            device_id_type=MESH,
+        )
+
+    X, Y, PAIR, DOWN, UP = range(5)
+    peers = (at_x, at_y, at_pair, at_down, at_up)
+
+    def either(full, visit):
+        if full is True:
+            visit(True)
+            return
+        pl.when(full)(lambda: visit(True))
+        pl.when(jnp.logical_not(full))(lambda: visit(False))
+
+    def wide(way, p):
+        if p < 2 or way == DOWN:
+            return True
+        return z + 1 < hot_levels if way == UP else hot
+
+    def send(s, p, way, own=False):
+        either(wide(way, p), lambda f: copy_of(s, p, f, way, peers[way], own).start())
+
+    def sent(s, p, way):
+        either(wide(way, p), lambda f: copy_of(s, p, f, way, peers[way]).wait_send())
+
+    def arrived(s, p, below=True):
+        full = hot if (p == 2 and below) else True
+        either(full, lambda f: copy_of(s, p, f, PAIR, at_pair).wait_recv())
+
+    pl.semaphore_wait(barrier, 1 + d % 2 + d // 2 + jnp.minimum(z, 1))
+
+    def tell(way):
+        pl.semaphore_signal(ready.at[way], inc=1, device_id=peers[way], device_id_type=MESH)
+
+    pl.when(low_x)(lambda: tell(X))
+    pl.when(low_y)(lambda: tell(Y))
+
+    @pl.when(low_z)
+    def _():
+        pl.semaphore_signal(ready.at[UP], inc=1, device_id=at_down, device_id_type=MESH)
+
+    def to_lower(p):
+        pl.when(low_z)(lambda: send(me, p, DOWN, True))
+        pl.when(low_x)(lambda: send(me, p, X, True))
+        pl.when(low_y)(lambda: send(me, p, Y, True))
+        send(me, p, PAIR, True)
+
+    to_lower(0)
+    to_lower(1)
+
     for copy in input_copies:
         copy.wait()
     names = -(-experts // TILE) * TILE
@@ -257,128 +338,122 @@
         return lax.dot_general(weights, unit, TN, preferred_element_type=f32)
 
     main_part, tail_part = turned(0), turned(LANES // 2)
-    slab[me, weight_at] = (main_part[:TILE] + tail_part[TILE:]).astype(bf16)
-    tok_tail = tok_ref[TILE:, :].astype(f32)[:8]
-    cot_tail = cot_ref[TILE:, :].astype(f32)[:8]
+    small[me, half] = (main_part[:TILE] + tail_part[TILE:]).astype(bf16)
+    tok_tail = tok_ref[...].astype(f32)[:8]
+    cot_tail = cot_ref[...].astype(f32)[:8]
     tail_row = lax.broadcasted_iota(jnp.int32, (8, features), 0)
     spill = jnp.where(tail_row < 4, tok_tail, pltpu.roll(cot_tail, 4, 0))
-    for j in range(blocks):
-        cols = slice(j * LANES, (j + 1) * LANES)
-        slab[me, j] = tok_ref[:TILE, cols]
-        slab[me, blocks + j] = cot_ref[:TILE, cols]
     for j in range(half):
         lo = spill[:, j * LANES : (j + 1) * LANES]
         hi = spill[:, (half + j) * LANES : (half + j + 1) * LANES]
-        slab[me, spill_at + j] = jnp.concatenate([lo, hi], axis=0).astype(bf16)
-
-    pl.semaphore_wait(barrier, 3 + levels - 1)
-
-    tiles = slab.shape[1]
-    cut = (tiles + 1) // 2
-    pieces = (pl.ds(0, cut), pl.ds(cut, tiles - cut))
-
-    def copy_of(s, p, way, peer):
-        return pltpu.make_async_remote_copy(
-            src_ref=slab.at[s, pieces[p]],
-            dst_ref=slab.at[s, pieces[p]],
-            send_sem=send_sem.at[way, p, s],
-            recv_sem=recv_sem.at[p, s],
-            device_id=peer,
-            device_id_type=MESH,
-        )
-
-    def to_x(s, p):
-        return copy_of(s, p, 0, to(dx, z, c))
-
-    def to_y(s, p):
-        return copy_of(s, p, 1, to(dy, z, c))
-
-    def to_pair(s, p):
-        return copy_of(s, p, 2, to(d, z, pc))
-
-    def to_level(p, step):
-        return copy_of(me, p, 2 + step, to(d, (z + step) % levels, c))
-
-    def arrived(s, p):
-        to_pair(s, p).wait_recv()
-
-    def at_distance(dist, visit):
+        small[me, j] = jnp.concatenate([lo, hi], axis=0).astype(bf16)
+
+    to_lower(2)
+
+    def to_upper(way, up):
+        @pl.when(up)
+        def _():
+            pl.semaphore_wait(ready.at[way], 1)
+            for p in range(3):
+                send(me, p, way, True)
+
+    to_upper(UP, up_z)
+    to_upper(X, up_x)
+    to_upper(Y, up_y)
+
+    def sides(dist, visit):
         if dist == 0:
             visit(z, 0)
             return
+        pl.when(z + dist < levels)(lambda: visit(z + dist, 1))
         pl.when(z - dist >= 0)(lambda: visit(z - dist, -1))
-        pl.when(z + dist < levels)(lambda: visit(z + dist, 1))
-
-    def column(dist, p):
-        def visit(level, side):
-            s = slab_id(d, level, c)
-            if side:
+
+    def column(dist):
+        for p in range(3):
+
+            def visit(level, side):
+                s = slab_id(d, level, c)
+                arrived(s, p, side < 0)
+                if side > 0:
+                    pl.when(low_z)(lambda: send(s, p, DOWN))
+                else:
+                    pl.when(up_z)(lambda: send(s, p, UP))
+                send(s, p, X)
+                send(s, p, Y)
+                send(s, p, PAIR)
+
+            sides(dist, visit)
+
+    def turn(dp_is_x, p):
+        if p < 2:
+            return p == (0 if dp_is_x else 1)
+        return c == (0 if dp_is_x else 1)
+
+    def onward(dp_is_x, p, act):
+        take = turn(dp_is_x, p)
+        way = Y if dp_is_x else X
+        if take is True:
+            act(way)
+        elif take is not False:
+            pl.when(take)(lambda: act(way))
+
+    def beside(dist):
+        for p in range(3):
+
+            def visit(level, side):
+                for dp, is_x in ((dx, True), (dy, False)):
+                    s = slab_id(dp, level, c)
+                    arrived(s, p)
+                    onward(is_x, p, lambda way: send(s, p, way))
+                    send(s, p, PAIR)
+
+            sides(dist, visit)
+
+    def across(dist):
+        for p in range(3):
+
+            def visit(level, side):
+                s = slab_id(dd, level, c)
                 arrived(s, p)
-            to_x(s, p).start()
-            to_y(s, p).start()
-            if side == 0:
-                for step in range(1, levels):
-                    to_level(p, step).start()
-            to_pair(s, p).start()
-
-        at_distance(dist, visit)
-
-    def beside(dist, p):
-        def visit(level, side):
-            for dp in (dx, dy):
-                s = slab_id(dp, level, c)
-                arrived(s, p)
-                if p == 0 and dp is dx:
-                    to_y(s, p).start()
-                if p == 1 and dp is dy:
-                    to_x(s, p).start()
-                to_pair(s, p).start()
-
-        at_distance(dist, visit)
-
-    def across(dist):
-        def visit(level, side):
-            s = slab_id(dd, level, c)
-            for p in (0, 1):
-                arrived(s, p)
-                to_pair(s, p).start()
-
-        at_distance(dist, visit)
+                send(s, p, PAIR)
+
+            sides(dist, visit)
 
     def from_pair(dp):
         for level in range(levels):
-            for p in (0, 1):
+            for p in range(3):
                 arrived(slab_id(dp, level, pc), p)
 
-    column(0, 0)
-    column(0, 1)
-    for dist in range(1, levels):
-        for p in (0, 1):
-            column(dist, p)
-    from_pair(d)
-
     main_rows = experts * TILE
-    group_rows = main_rows + experts * 8
+    spill_rows = experts // 2 * 8
+    group_rows = main_rows + spill_rows
     main_lane = lax.broadcasted_iota(jnp.int32, (main_rows, LANES), 1)
-    tail_lane = lax.broadcasted_iota(jnp.int32, (experts * 8, LANES), 1)
+    tail_lane = lax.broadcasted_iota(jnp.int32, (spill_rows, LANES), 1)
+    first_w = lax.broadcasted_iota(jnp.int32, (spill_rows, LANES), 0) % 8 < 4
+    first = lax.broadcasted_iota(jnp.int32, (spill_rows, features), 0) % 8 < 4
 
     def group(dp, at):
         rows = pl.ds(at, group_rows)
         part = pl.ds(dp * experts, experts)
-
-        def main(j):
-            return slab[part, j].reshape(main_rows, LANES)
-
-        lo, hi = [], []
+        lo_a, lo_b, hi_a, hi_b = [], [], [], []
         for j in range(half):
-            both = slab[part, spill_at + j].astype(f32)
-            lo.append(both[:, :8].reshape(experts * 8, LANES))
-            hi.append(both[:, 8:].reshape(experts * 8, LANES))
-        tail = jnp.concatenate(lo + hi, axis=1)
-        cot_rows = pltpu.roll(tail, experts * 8 - 4, 0)
-        w_all = slab[part, weight_at].astype(f32)
+            both = small[part, j].astype(f32)
+            low, high = both[:, :8], both[:, 8:]
+            lo_a.append(low[: experts // 2].reshape(spill_rows, LANES))
+            lo_b.append(low[experts // 2 :].reshape(spill_rows, LANES))
+            hi_a.append(high[: experts // 2].reshape(spill_rows, LANES))
+            hi_b.append(high[experts // 2 :].reshape(spill_rows, LANES))
+        tail_a = jnp.concatenate(lo_a + hi_a, axis=1)
+        tail_b = jnp.concatenate(lo_b + hi_b, axis=1)
+        tok_rows = jnp.where(first, tail_a, pltpu.roll(tail_b, 4, 0))
+        cot_rows = jnp.where(first, pltpu.roll(tail_a, spill_rows - 4, 0), tail_b)
+        tok_rows = jnp.where(hot, tok_rows, 0.0)
+        cot_rows = jnp.where(hot, cot_rows, 0.0)
+        w_all = small[part, half].astype(f32)
         w_main = w_all.reshape(main_rows, LANES)
-        w_tail = w_all[:, :8].reshape(experts * 8, LANES)
+        w_a = w_all[: experts // 2, :8].reshape(spill_rows, LANES)
+        w_b = w_all[experts // 2 :, :8].reshape(spill_rows, LANES)
+        w_tail = jnp.where(first_w, w_a, pltpu.roll(w_b, 4, 0))
         w = jnp.concatenate(
             [
                 jnp.sum(jnp.where(main_lane == e, w_main, 0.0), axis=1, keepdims=True),
@@ -387,14 +462,10 @@
             axis=0,
         )
         all_t[rows, :] = jnp.concatenate(
-            [jnp.concatenate([main(j) for j in range(blocks)], axis=1), tail.astype(bf16)], axis=0
+            [all_tok[part].reshape(main_rows, features), tok_rows.astype(bf16)], axis=0
         )
         cot = jnp.concatenate(
-            [
-                jnp.concatenate([main(blocks + j) for j in range(blocks)], axis=1).astype(f32),
-                cot_rows,
-            ],
-            axis=0,
+            [all_cot[part].reshape(main_rows, features).astype(f32), cot_rows], axis=0
         )
         all_og[rows, :] = (w * cot).astype(bf16)
         t = all_t[rows, :]
@@ -409,64 +480,92 @@
         )
         all_ug[rows, :] = (hidden_grad * act).astype(bf16)
 
+    for copy in own_copies:
+        copy.wait()
+    column(1)
+    beside(0)
+    column(2)
+    beside(1)
+    column(3)
+    from_pair(d)
     for copy in weight_copies:
         copy.wait()
     group(d, 0)
+    beside(2)
     own = pl.ds(0, group_rows)
     rg = lax.dot_general(all_gg[own, :], wg[...], NT, preferred_element_type=f32)
     rg = rg + lax.dot_general(all_ug[own, :], wu[...], NT, preferred_element_type=f32)
-    for j in range(blocks):
-        row_out[:, j] = (
-            rg[:main_rows, j * LANES : (j + 1) * LANES].reshape(experts, TILE, LANES).astype(bf16)
-        )
+    row_main[...] = rg[:main_rows].reshape(experts, TILE, features).astype(bf16)
     for j in range(half):
-        lo = rg[main_rows:, j * LANES : (j + 1) * LANES].reshape(experts, 8, LANES)
-        hi = rg[main_rows:, (half + j) * LANES : (half + j + 1) * LANES].reshape(experts, 8, LANES)
-        row_out[:, blocks + j] = jnp.concatenate([lo, hi], axis=1).astype(bf16)
+        lo = rg[main_rows:, j * LANES : (j + 1) * LANES].reshape(experts // 2, 8, LANES)
+        hi = rg[main_rows:, (half + j) * LANES : (half + j + 1) * LANES].reshape(
+            experts // 2, 8, LANES
+        )
+        row_tail[:, j] = jnp.concatenate([lo, hi], axis=1).astype(bf16)
 
     def pair_copy(level):
         return pltpu.make_async_remote_copy(
-            src_ref=row_out.at[level * 2 + pc],
-            dst_ref=pair_in.at[level],
+            src_ref=row_main.at[level * 2 + pc],
+            dst_ref=pair_main.at[level],
             send_sem=pair_send.at[level],
             recv_sem=pair_recv.at[level],
-            device_id=to(d, z, pc),
+            device_id=at_pair,
+            device_id_type=MESH,
+        )
+
+    def pair_tail_copy(k):
+        return pltpu.make_async_remote_copy(
+            src_ref=row_tail.at[k * 2 + pc],
+            dst_ref=pair_tail.at[k],
+            send_sem=pair_send.at[levels + k],
+            recv_sem=pair_recv.at[levels + k],
+            device_id=at_pair,
             device_id_type=MESH,
         )
 
     for level in range(levels):
         pair_copy(level).start()
 
-    for dist in range(levels):
-        for p in (0, 1):
-            beside(dist, p)
-
+    @pl.when(hot)
+    def _():
+        for k in range(hot_levels):
+            pair_tail_copy(k).start()
+
+    beside(3)
     for level in range(levels):
         pair_copy(level).wait_recv()
-        pair_sum[level] = (
-            row_out[level * 2 + c].astype(f32) + pair_in[level].astype(f32)
+        sum_main[level] = (
+            row_main[level * 2 + c].astype(f32) + pair_main[level].astype(f32)
         ).astype(bf16)
 
-    def z_copy(step):
+    @pl.when(hot)
+    def _():
+        for k in range(hot_levels):
+            pair_tail_copy(k).wait_recv()
+            sum_tail[k] = (
+                row_tail[k * 2 + c].astype(f32) + pair_tail[k].astype(f32)
+            ).astype(bf16)
+
+    def z_copy(step, tail):
         level = (z + step) % levels
+        src, dst = (sum_tail, z_tail) if tail else (sum_main, z_main)
         return pltpu.make_async_remote_copy(
-            src_ref=pair_sum.at[level],
-            dst_ref=z_in.at[step - 1],
-            send_sem=z_send.at[step - 1],
-            recv_sem=z_recv.at[step - 1],
-            device_id=to(d, level, c),
+            src_ref=src.at[level % hot_levels if tail else level],
+            dst_ref=dst.at[step - 1],
+            send_sem=z_send.at[tail, step - 1],
+            recv_sem=z_recv.at[tail, step - 1],
+            device_id=(d, level * 2 + c),
             device_id_type=MESH,
         )
 
     for step in range(1, levels):
-        z_copy(step).start()
+        z_copy(step, 0).start()
+        pl.when(hot)(lambda: z_copy(step, 1).start())
 
     from_pair(dx)
     group(dx, group_rows)
     from_pair(dy)
     group(dy, 2 * group_rows)
-    for dist in range(levels):
-        across(dist)
     share = features // 4
 
     def weight_terms(at, count):
@@ -478,6 +577,8 @@
             lax.dot_general(all_h[rows, :], all_og[rows, :], TN, preferred_element_type=f32),
         )
 
+    for dist in range(levels):
+        across(dist)
     early = weight_terms(0, 3 * group_rows)
     acc_gate[...], acc_up[...], acc_down[...] = early
     from_pair(dd)
@@ -487,37 +588,47 @@
     gu_out[0] = (acc_up[...] + late[1]).astype(bf16)
     gd_out[0] = (acc_down[...] + late[2]).astype(bf16)
 
-    total = pair_sum[z].astype(f32)
+    total = sum_main[z].astype(f32)
+    spilled = jnp.where(hot, sum_tail[z % hot_levels].astype(f32), 0.0)
     for step in range(1, levels):
-        z_copy(step).wait_recv()
-        total = total + z_in[step - 1].astype(f32)
-    for j in range(blocks):
-        tg_ref[:TILE, j * LANES : (j + 1) * LANES] = total[j].astype(bf16)
+        z_copy(step, 0).wait_recv()
+        total = total + z_main[step - 1].astype(f32)
+        from_hot = (z + levels - step) % levels < hot_levels
+        pl.when(from_hot)(lambda: z_copy(step, 1).wait_recv())
+        spilled = spilled + jnp.where(from_hot, z_tail[step - 1].astype(f32), 0.0)
+    tg_ref[:TILE, :] = total.astype(bf16)
+    kept_row = lax.broadcasted_iota(jnp.int32, (8, LANES), 0) < 4
     blank = jnp.zeros((8, LANES), f32)
     for j in range(half):
-        tile = total[blocks + j]
-        tg_ref[TILE:, j * LANES : (j + 1) * LANES] = jnp.concatenate(
-            [tile[:8], blank], axis=0
-        ).astype(bf16)
-        tg_ref[TILE:, (half + j) * LANES : (half + j + 1) * LANES] = jnp.concatenate(
-            [tile[8:], blank], axis=0
-        ).astype(bf16)
+        for at, rows in ((j, spilled[j][:8]), (half + j, spilled[j][8:])):
+            rows = jnp.where(hot, rows, pltpu.roll(rows, 4, 0))
+            tg_ref[TILE:, at * LANES : (at + 1) * LANES] = jnp.concatenate(
+                [jnp.where(kept_row, rows, 0.0), blank], axis=0
+            ).astype(bf16)
 
     for level in range(levels):
         pair_copy(level).wait_send()
-        to_y(slab_id(dx, level, c), 0).wait_send()
-        to_x(slab_id(dy, level, c), 1).wait_send()
-        s = slab_id(d, level, c)
-        for p in (0, 1):
-            to_x(s, p).wait_send()
-            to_y(s, p).wait_send()
+    for step in range(1, levels):
+        z_copy(step, 0).wait_send()
+
+    @pl.when(hot)
+    def _():
+        for k in range(hot_levels):
+            pair_tail_copy(k).wait_send()
+        for step in range(1, levels):
+            z_copy(step, 1).wait_send()
+
+    for p in range(3):
+        for level in range(levels):
+            s = slab_id(d, level, c)
+            sent(s, p, X)
+            sent(s, p, Y)
             for dp in (d, dx, dy, dd):
-                to_pair(slab_id(dp, level, c), p).wait_send()
-
-    for step in range(1, levels):
-        z_copy(step).wait_send()
-        to_level(0, step).wait_send()
-        to_level(1, step).wait_send()
+                sent(slab_id(dp, level, c), p, PAIR)
+            for dp, is_x in ((dx, True), (dy, False)):
+                onward(is_x, p, lambda way: sent(slab_id(dp, level, c), p, way))
+            pl.when(jnp.logical_and(level >= z, z > 0))(lambda: sent(s, p, DOWN))
+            pl.when(jnp.logical_and(level <= z, z < levels - 1))(lambda: sent(s, p, UP))
 
 
 def write_kernel(*refs):
@@ -537,11 +648,10 @@
     replicas = lax.axis_size("dp")
     token_count, features = tokens.shape
     hidden_size = w_gate.shape[2]
-    blocks = features // LANES
+    half = features // LANES // 2
     levels = experts // 2
-    tiles = 2 * blocks + blocks // 2 + 1
-    back = blocks + blocks // 2
-    rows = replicas * experts * (TILE + 8)
+    slots = replicas * experts
+    rows = slots * (TILE + 4)
     bf16 = jnp.bfloat16
     vmem = pl.BlockSpec(memory_space=pltpu.VMEM)
     hbm = pl.BlockSpec(memory_space=pltpu.HBM)
@@ -571,14 +681,16 @@
         in_specs=[hbm] * 9,
         out_specs=(vmem, vmem, vmem, vmem),
         scratch_shapes=[
-            pltpu.VMEM(tokens.shape, bf16),
-            pltpu.VMEM(tokens.shape, bf16),
+            pltpu.VMEM((TILE, features), bf16),
+            pltpu.VMEM((TILE, features), bf16),
             pltpu.VMEM(routes.shape[::-1], jnp.int32),
             pltpu.VMEM(routes.shape[::-1], bf16),
             pltpu.SMEM(hot_experts.shape, jnp.int32),
             pltpu.SMEM(hot_experts.shape, jnp.int32),
             dma((6,)),
-            pltpu.VMEM((replicas * experts, tiles, TILE, LANES), bf16),
+            pltpu.VMEM((slots, TILE, features), bf16),
+            pltpu.VMEM((slots, TILE, features), bf16),
+            pltpu.VMEM((slots, half + 1, TILE, LANES), bf16),
             pltpu.VMEM((features, hidden_size), bf16),
             pltpu.VMEM((features, hidden_size), bf16),
             pltpu.VMEM((hidden_size, features), bf16),
@@ -590,17 +702,23 @@
             pltpu.VMEM((features // replicas, hidden_size), jnp.float32),
             pltpu.VMEM((features // replicas, hidden_size), jnp.float32),
             pltpu.VMEM((hidden_size, features), jnp.float32),
-            pltpu.VMEM((experts, back, TILE, LANES), bf16),
-            pltpu.VMEM((levels, back, TILE, LANES), bf16),
-            pltpu.VMEM((levels, back, TILE, LANES), bf16),
-            pltpu.VMEM((levels - 1, back, TILE, LANES), bf16),
+            pltpu.VMEM((experts, TILE, features), bf16),
+            pltpu.VMEM((experts // 2, half, TILE, LANES), bf16),
+            pltpu.VMEM((levels, TILE, features), bf16),
+            pltpu.VMEM((levels // 2, half, TILE, LANES), bf16),
+            pltpu.VMEM((levels, TILE, features), bf16),
+            pltpu.VMEM((levels // 2, half, TILE, LANES), bf16),
+            pltpu.VMEM((levels - 1, TILE, features), bf16),
+            pltpu.VMEM((levels - 1, half, TILE, LANES), bf16),
             dma((3,)),
-            dma((levels + 2, 2, replicas * experts)),
-            dma((2, replicas * experts)),
-            dma((levels,)),
-            dma((levels,)),
-            dma((levels - 1,)),
-            dma((levels - 1,)),
+            dma((2,)),
+            dma((5, 3, slots)),
+            dma((3, slots)),
+            dma((levels + levels // 2,)),
+            dma((levels + levels // 2,)),
+            dma((2, levels - 1)),
+            dma((2, levels - 1)),
+            pltpu.SemaphoreType.REGULAR((5,)),
         ],
         compiler_params=pltpu.CompilerParams(
             collective_id=0, has_side_effects=True, vmem_limit_bytes=32 * 1024 * 1024

time: 30.1 us -> 30 us (level)
  no operation moved by 1% of the time
where the time goes in v1:
time: 30 us; the launch traced here: 29.8 us
  Pallas kernels  29.2 us (97%)
  between operations  0.64 us (2%)
    pallas_call x1, Pallas kernels, dense_shards(): pl.pallas_call(functools.partial(dense_kernel, experts), out_shape=(jax.S...  28.1 us
    pallas_call x1, Pallas kernels, dense_shards(): pl.pallas_call(write_kernel, out_shape=tuple((jax.ShapeDtypeStruct(r.shap...  1.07 us

profile of v1, /device:TPU:0, one launch (start us, length us, event | category | flops | bytes accessed | tf_op | source)
XLA Modules:
  0.0 29.8 jit_solution(10246111209310431976)
XLA Ops:
  0.6 28.1 %shard_map.120 = (bf16[32,1024]{1,0:T(8,128)(2,1)S(1)}, bf16[1,256,384]{2,1,0:T(8,128)(2,1)S(1)}, bf16[1,256,384]{2,1,0:T(8,128)(2,1)S(1)}, bf16[1,384,1024]{2,1,0:T(8,128)(2,1)S(1)}) custom-call(bf16[32,1024]{1,0:T(8,128)(2,1)} %tok_hbm.1, bf16[32,1024]{1,0:T(8,128)(2,1)} %cot_hbm.1, s32[8,32]{1,0:T(8,128)} %bitcast.2, bf16[8,32]{1,0:T(8,128)(2,1)} %bitcast.3, ...), custom_call_target="tpu_custom_call" | custom-call | tf_op jit(solution)/shard_map/pallas_call | solution.py:673
  28.8 1.1 %shard_map.121 = (bf16[32,1024]{1,0:T(8,128)(2,1)}, bf16[1,256,384]{2,1,0:T(8,128)(2,1)}, bf16[1,256,384]{2,1,0:T(8,128)(2,1)}, bf16[1,384,1024]{2,1,0:T(8,128)(2,1)}) custom-call(bf16[32,1024]{1,0:T(8,128)(2,1)S(1)} %get-tuple-element.8.refs_0_, bf16[1,256,384]{2,1,0:T(8,128)(2,1)S(1)} %get-tuple-element.9.refs_1_, ...), custom_call_target="tpu_custom_call" | custom-call | tf_op jit(solution)/shard_map/pallas_call | solution.py:727

commit v2 on v0

v2 whole, which is shorter than its diff:
```python
import functools

import jax
import jax.numpy as jnp
from jax import lax
from jax.experimental import pallas as pl
from jax.experimental.pallas import tpu as pltpu
from jax.sharding import PartitionSpec as P


def forward_rows(weight_gate, weight_up, weight_down, row_tokens, row_cotan, row_weights):
    gate_pre = jnp.dot(row_tokens, weight_gate, preferred_element_type=jnp.float32)
    up_proj = jnp.dot(row_tokens, weight_up, preferred_element_type=jnp.float32)
    sigmoid_gate = jax.nn.sigmoid(gate_pre)
    gate_act = gate_pre * sigmoid_gate
    hidden = (gate_act * up_proj).astype(jnp.bfloat16)
    out_grad = (row_weights.astype(jnp.float32)[:, None] * row_cotan.astype(jnp.float32)).astype(
        jnp.bfloat16
    )
    hidden_grad = jnp.dot(out_grad, weight_down.T, preferred_element_type=jnp.float32)
    gate_grad = (
        hidden_grad * up_proj * sigmoid_gate * (1.0 + gate_pre * (1.0 - sigmoid_gate))
    ).astype(jnp.bfloat16)
    up_grad = (hidden_grad * gate_act).astype(jnp.bfloat16)
    row_grads = jnp.dot(gate_grad, weight_gate.T, preferred_element_type=jnp.float32)
    row_grads = row_grads + jnp.dot(up_grad, weight_up.T, preferred_element_type=jnp.float32)
    return (row_grads.astype(jnp.bfloat16), (row_tokens, gate_grad, up_grad, hidden, out_grad))


def weight_terms(pieces):
    row_tokens, gate_grad, up_grad, hidden, out_grad = pieces
    grad_gate = jnp.dot(row_tokens.T, gate_grad, preferred_element_type=jnp.float32)
    grad_up = jnp.dot(row_tokens.T, up_grad, preferred_element_type=jnp.float32)
    grad_down = jnp.dot(hidden.T, out_grad, preferred_element_type=jnp.float32)
    return (grad_gate, grad_up, grad_down)


def expert_pass(weight_gate, weight_up, weight_down, row_tokens, row_cotan, row_weights):
    row_grads, pieces = forward_rows(
        weight_gate, weight_up, weight_down, row_tokens, row_cotan, row_weights
    )
    return (row_grads, weight_terms(pieces))


def shards(tokens, cotangent, routes, combine, hot_experts, extra_slots, w_gate, w_up, w_down):
    expert_count = lax.axis_size("expert")
    token_count, features = tokens.shape
    route_count = routes.shape[1]
    capacity = max(2, min(token_count * route_count * 7 // (8 * expert_count), token_count // 2))
    spare_slots = 2 * max(1, capacity // 6)
    expert_ids = routes.reshape(-1)
    assign_count = expert_ids.shape[0]
    assign_order = jnp.arange(assign_count, dtype=jnp.int32)
    earlier = (expert_ids[:, None] == expert_ids[None, :]) & (
        assign_order[None, :] < assign_order[:, None]
    )
    slot_rank = jnp.sum(earlier.astype(jnp.int32), axis=1)
    hot_match = expert_ids[:, None] == hot_experts[None, :]
    slot_limit = capacity + jnp.sum(jnp.where(hot_match, extra_slots[None, :], 0), axis=1)
    is_kept = slot_rank < slot_limit
    slot_count = capacity + spare_slots
    total_slots = expert_count * slot_count
    flat_slot = jnp.where(is_kept, expert_ids * slot_count + slot_rank, total_slots)
    slot_ids = jnp.arange(total_slots, dtype=jnp.int32)
    assign_onehot = slot_ids[:, None] == flat_slot[None, :]
    token_onehot = jnp.any(
        assign_onehot.reshape(total_slots, token_count, route_count), axis=2
    ).astype(jnp.bfloat16)
    both_rows = jnp.concatenate([tokens, cotangent], axis=1)
    filled = jnp.dot(token_onehot, both_rows, preferred_element_type=jnp.float32).astype(
        jnp.bfloat16
    )
    token_send = filled[:, :features].reshape(expert_count, slot_count, features)
    cotan_send = filled[:, features:].reshape(expert_count, slot_count, features)
    weight_flat = jnp.sum(
        jnp.where(assign_onehot, combine.reshape(-1).astype(jnp.float32)[None, :], 0.0), axis=1
    )
    weight_send = weight_flat.astype(jnp.bfloat16).reshape(expert_count, slot_count)
    token_recv, cotan_recv, weight_recv = (
        lax.all_to_all(token_send, "expert", split_axis=0, concat_axis=0, tiled=True),
        lax.all_to_all(cotan_send, "expert", split_axis=0, concat_axis=0, tiled=True),
        lax.all_to_all(weight_send, "expert", split_axis=0, concat_axis=0, tiled=True),
    )
    own_weights = (w_gate[0], w_up[0], w_down[0])
    all_rows, grad_terms = expert_pass(
        own_weights[0],
        own_weights[1],
        own_weights[2],
        token_recv.reshape(-1, features),
        cotan_recv.reshape(-1, features),
        weight_recv.reshape(-1),
    )
    grad_rows = all_rows.reshape(expert_count, slot_count, features)
    returned_rows = lax.all_to_all(grad_rows, "expert", split_axis=0, concat_axis=0, tiled=True)
    token_grads = jnp.dot(
        token_onehot.T,
        returned_rows.reshape(total_slots, features),
        preferred_element_type=jnp.float32,
    ).astype(jnp.bfloat16)
    grad_gate, grad_up = (
        lax.psum_scatter(grad_terms[0][None], "dp", scatter_dimension=1, tiled=True),
        lax.psum_scatter(grad_terms[1][None], "dp", scatter_dimension=1, tiled=True),
    )
    grad_down = lax.psum(grad_terms[2][None], "dp")
    return (
        token_grads,
        grad_gate.astype(jnp.bfloat16),
        grad_up.astype(jnp.bfloat16),
        grad_down.astype(jnp.bfloat16),
    )


MESH = pl.DeviceIdType.MESH
LANES = 128
TILE = 16
NT = (((1,), (1,)), ((), ()))
TN = (((0,), (0,)), ((), ()))


def slots_of(token_count, route_count, expert_count):
    capacity = max(2, min(token_count * route_count * 7 // (8 * expert_count), token_count // 2))
    return capacity, 2 * max(1, capacity // 6)


def dense_fits(sizes, token_count, features, route_count, hidden_size):
    capacity, spare = slots_of(token_count, route_count, sizes["expert"])
    return (
        route_count == sizes["expert"]
        and sizes["dp"] == 4
        and sizes["expert"] == 8
        and token_count == 2 * TILE
        and capacity == TILE
        and spare * 2 == 8
        and features % (8 * LANES) == 0
        and hidden_size % LANES == 0
    )


def dense_kernel(
    experts,
    tok_hbm,
    cot_hbm,
    routes_hbm,
    comb_hbm,
    hot_hbm,
    extra_hbm,
    wg_hbm,
    wu_hbm,
    wd_hbm,
    tg_ref,
    acc_gate,
    acc_up,
    acc_down,
    late_cols,
    late_og,
    late_h,
    late_gg,
    late_ug,
    tok_ref,
    cot_ref,
    routes_ref,
    comb_ref,
    hot_ref,
    extra_ref,
    all_tok,
    slab,
    wg,
    wu,
    wd,
    all_t,
    all_og,
    all_h,
    all_gg,
    all_ug,
    late_t,
    row_out,
    pair_in,
    row_sum,
    z_in,
    in_sem,
    w_sem,
    flat_send,
    down_send,
    up_send,
    recv_sem,
    pair_recv,
    row_sem,
    z_send,
    z_recv,
    ready,
):
    levels = experts // 2
    hot_levels = levels // 2
    features = all_tok.shape[2]
    blocks = features // LANES
    half = blocks // 2
    weight_at, spill_at = blocks, blocks + 1
    bf16, f32 = jnp.bfloat16, jnp.float32

    d = lax.axis_index("dp")
    e = lax.axis_index("expert")
    z, c = e // 2, e % 2
    dx = d + 1 - 2 * (d % 2)
    dy = (d + 2) % 4
    dd = 3 - d
    pc = 1 - c
    upper_half = z // 2
    near, far = 2 * upper_half, 2 - 2 * upper_half
    hot = z < hot_levels
    low_x, low_y, low_z = d % 2 == 1, d // 2 == 1, z > 0
    up_x, up_y, up_z = d % 2 == 0, d // 2 == 0, z < levels - 1
    at_x, at_y, at_pair = (dx, e), (dy, e), (d, z * 2 + pc)
    at_below, at_above = (d, jnp.maximum(e - 2, 0)), (d, jnp.minimum(e + 2, experts - 1))

    def slot(dp, level, core):
        return (dp * 2 + core) * levels + level

    me = slot(d, z, c)
    input_copies = [
        pltpu.make_async_copy(h, v, in_sem.at[i])
        for i, (h, v) in enumerate(
            (
                (tok_hbm.at[pl.ds(TILE, TILE)], tok_ref),
                (cot_hbm, cot_ref),
                (routes_hbm, routes_ref),
                (comb_hbm, comb_ref),
                (hot_hbm, hot_ref),
                (extra_hbm, extra_ref),
                (tok_hbm.at[pl.ds(0, TILE)], all_tok.at[me]),
            )
        )
    ]
    own_tokens = input_copies.pop()
    weight_copies = [
        pltpu.make_async_copy(h.at[0], v, w_sem.at[i])
        for i, (h, v) in enumerate(((wg_hbm, wg), (wu_hbm, wu), (wd_hbm, wd)))
    ]

    barrier = pltpu.get_barrier_semaphore()

    def greet(peer):
        pl.semaphore_signal(barrier, inc=1, device_id=peer, device_id_type=MESH)

    greet(at_pair)
    pl.when(up_x)(lambda: greet(at_x))
    pl.when(up_y)(lambda: greet(at_y))
    pl.when(up_z)(lambda: greet(at_above))
    for copy in input_copies + [own_tokens] + weight_copies:
        copy.start()

    def piece(s, p, full):
        if p == 0:
            return all_tok.at[s]
        return slab.at[s] if full else slab.at[s, pl.ds(0, spill_at)]

    def either(full, visit):
        if full is True or full is False:
            visit(full)
            return
        pl.when(full)(lambda: visit(True))
        pl.when(jnp.logical_not(full))(lambda: visit(False))

    def remote(src, dst, send, recv, peer):
        return pltpu.make_async_remote_copy(
            src_ref=src,
            dst_ref=dst,
            send_sem=send,
            recv_sem=recv,
            device_id=peer,
            device_id_type=MESH,
        )

    def push(dp, level, p, full, send, peer, own=False):
        s = slot(dp, level, c)

        def go(f):
            dst = piece(s, p, f)
            src = tok_hbm.at[pl.ds(0, TILE)] if own and p == 0 else dst
            remote(src, dst, send, recv_sem.at[p, dp * levels + level], peer).start()

        either(True if p == 0 else full, go)

    X, Y, PAIR = range(3)

    def to_x(dp, level, p, own=False):
        push(dp, level, p, hot, flat_send.at[X, p], at_x, own)

    def to_y(dp, level, p, own=False):
        push(dp, level, p, hot, flat_send.at[Y, p], at_y, own)

    def to_above(level, p, own=False):
        push(d, level, p, z + 1 < hot_levels, up_send.at[p, level], at_above, own)

    def to_below(level, p, own=False):
        push(d, level, p, True, down_send.at[p, level - 1], at_below, own)

    def to_pair(dp, level, p, bank, own=False):
        s = slot(dp, level, c)

        def go(f):
            dst = piece(s, p, f)
            src = tok_hbm.at[pl.ds(0, TILE)] if own and p == 0 else dst
            remote(src, dst, flat_send.at[PAIR, p], pair_recv.at[p, bank], at_pair).start()

        either(True if p == 0 else hot, go)

    def arrived(dp, level, p, above=False):
        s = slot(dp, level, c)

        def go(f):
            dst = piece(s, p, f)
            at = recv_sem.at[p, dp * levels + level]
            remote(dst, dst, flat_send.at[X, p], at, at_x).wait_recv()

        either(True if p == 0 or above else hot, go)

    pl.semaphore_wait(barrier, 1 + d % 2 + d // 2 + jnp.minimum(z, 1))

    def tell(way, peer):
        pl.semaphore_signal(ready.at[way], inc=1, device_id=peer, device_id_type=MESH)

    pl.when(low_x)(lambda: tell(0, at_x))
    pl.when(low_y)(lambda: tell(1, at_y))
    pl.when(low_z)(lambda: tell(2, at_below))

    OWN, NEAR, FAR, DD_NEAR, DD_FAR = range(5)

    def to_lower(p):
        pl.when(low_z)(lambda: to_below(z, p, True))
        pl.when(low_x)(lambda: to_x(d, z, p, True))
        pl.when(low_y)(lambda: to_y(d, z, p, True))
        to_pair(d, z, p, OWN, True)

    to_lower(0)

    for copy in input_copies:
        copy.wait()
    names = -(-experts // TILE) * TILE
    expert_row = lax.broadcasted_iota(jnp.int32, (names, 2 * TILE), 0)
    token_lane = lax.broadcasted_iota(jnp.int32, (names, 2 * TILE), 1)
    routes = routes_ref[...]
    comb = comb_ref[...].astype(f32)
    weights = jnp.zeros((names, 2 * TILE), f32)
    for r in range(routes.shape[0]):
        weights = jnp.where(expert_row == routes[r : r + 1, :], comb[r : r + 1, :], weights)
    limit = jnp.full((names, 2 * TILE), TILE, jnp.int32)
    for j in range(hot_ref.shape[0]):
        limit = limit + jnp.where(expert_row == hot_ref[j], extra_ref[j], 0)
    weights = jnp.where(token_lane < limit, weights, 0.0).astype(bf16)
    unit_row = lax.broadcasted_iota(jnp.int32, (names, LANES), 0)
    unit_lane = lax.broadcasted_iota(jnp.int32, (names, LANES), 1)

    def turned(shift):
        unit = jnp.where(unit_lane == unit_row + shift, 1.0, 0.0).astype(bf16)
        return lax.dot_general(weights, unit, TN, preferred_element_type=f32)

    main_part, tail_part = turned(0), turned(LANES // 2)
    slab[me, weight_at] = (main_part[:TILE] + tail_part[TILE:]).astype(bf16)
    tok_tail = tok_ref[...].astype(f32)[:8]
    cot_tail = cot_ref[TILE:, :].astype(f32)[:8]
    tail_row = lax.broadcasted_iota(jnp.int32, (8, features), 0)
    spill = jnp.where(tail_row < 4, tok_tail, pltpu.roll(cot_tail, 4, 0))
    for j in range(blocks):
        slab[me, j] = cot_ref[:TILE, j * LANES : (j + 1) * LANES]
    for j in range(half):
        lo = spill[:, j * LANES : (j + 1) * LANES]
        hi = spill[:, (half + j) * LANES : (half + j + 1) * LANES]
        slab[me, spill_at + j] = jnp.concatenate([lo, hi], axis=0).astype(bf16)

    to_lower(1)

    def to_upper(way, up, act):
        @pl.when(up)
        def _():
            pl.semaphore_wait(ready.at[way], 1)
            for p in range(2):
                act(p)

    to_upper(2, up_z, lambda p: to_above(z, p, True))
    to_upper(0, up_x, lambda p: to_x(d, z, p, True))
    to_upper(1, up_y, lambda p: to_y(d, z, p, True))
    own_tokens.wait()

    def at_distance(dist, visit):
        if dist == 0:
            visit(z, 0)
            return
        pl.when(z + dist < levels)(lambda: visit(z + dist, 1))
        pl.when(z - dist >= 0)(lambda: visit(z - dist, -1))

    def bank_of(level):
        return (level // 2 + upper_half) % 2

    def column(dist):
        for p in range(2):

            def visit(level, side):
                arrived(d, level, p, side > 0)
                if side > 0:
                    pl.when(low_z)(lambda: to_below(level, p))
                else:
                    pl.when(up_z)(lambda: to_above(level, p))
                to_x(d, level, p)
                to_y(d, level, p)
                to_pair(d, level, p, OWN)

            at_distance(dist, visit)

    def beside(dist):
        for p in range(2):

            def visit(level, side):
                bank = NEAR + bank_of(level)
                arrived(dx, level, p)
                pl.when((p + c) % 2 == 0)(lambda: to_y(dx, level, p))
                to_pair(dx, level, p, bank)
                arrived(dy, level, p)
                pl.when((p + c) % 2 == 1)(lambda: to_x(dy, level, p))
                to_pair(dy, level, p, bank)

            at_distance(dist, visit)

    def across(dist):
        for p in range(2):

            def visit(level, side):
                arrived(dd, level, p)
                to_pair(dd, level, p, DD_NEAR + bank_of(level))

            at_distance(dist, visit)

    def from_pair(bank, at, count):
        region = pl.ds(at, count)
        remote(
            all_tok.at[region],
            all_tok.at[region],
            flat_send.at[PAIR, 0],
            pair_recv.at[0, bank],
            at_pair,
        ).wait_recv()

        def go(f):
            part = slab.at[region] if f else slab.at[region, pl.ds(0, spill_at)]
            remote(
                part, part, flat_send.at[PAIR, 1], pair_recv.at[1, bank], at_pair
            ).wait_recv()

        either(hot, go)

    def group(parts, store):
        each = sum(n for _, _, n in parts)
        main_rows, spill_rows = 2 * each * TILE, each * 8

        def slots_of_core(core):
            return [pl.ds(slot(dp, level, core), n) for dp, level, n in parts]

        lanes_a, lanes_b = slots_of_core(0), slots_of_core(1)

        def rows_of(at, lanes):
            return [slab[r, at] for r in lanes]

        def low8(lanes, at, cut):
            return jnp.concatenate(
                [v.astype(f32)[:, cut : cut + 8].reshape(-1, LANES) for v in rows_of(at, lanes)],
                axis=0,
            )

        def tail_of(lanes):
            return jnp.concatenate(
                [low8(lanes, spill_at + j, 0) for j in range(half)]
                + [low8(lanes, spill_at + j, 8) for j in range(half)],
                axis=1,
            )

        tail_a, tail_b = tail_of(lanes_a), tail_of(lanes_b)
        first = lax.broadcasted_iota(jnp.int32, (spill_rows, features), 0) % 8 < 4
        first_w = lax.broadcasted_iota(jnp.int32, (spill_rows, LANES), 0) % 8 < 4
        tok_rows = jnp.where(first, tail_a, pltpu.roll(tail_b, 4, 0))
        cot_rows = jnp.where(first, pltpu.roll(tail_a, spill_rows - 4, 0), tail_b)
        tok_rows = jnp.where(hot, tok_rows, 0.0)
        cot_rows = jnp.where(hot, cot_rows, 0.0)

        def main_of(at):
            return jnp.concatenate(
                [v.reshape(-1, LANES) for v in rows_of(at, lanes_a + lanes_b)], axis=0
            )

        w_main = main_of(weight_at).astype(f32)
        w_tail = jnp.where(
            first_w, low8(lanes_a, weight_at, 0), pltpu.roll(low8(lanes_b, weight_at, 0), 4, 0)
        )
        main_lane = lax.broadcasted_iota(jnp.int32, (main_rows, LANES), 1)
        tail_lane = lax.broadcasted_iota(jnp.int32, (spill_rows, LANES), 1)
        w = jnp.concatenate(
            [
                jnp.sum(jnp.where(main_lane == e, w_main, 0.0), axis=1, keepdims=True),
                jnp.sum(jnp.where(tail_lane == e + LANES // 2, w_tail, 0.0), axis=1, keepdims=True),
            ],
            axis=0,
        )
        t_ref, og_ref, h_ref, gg_ref, ug_ref, at = store
        rows = pl.ds(at, main_rows + spill_rows)
        t_ref[rows, :] = jnp.concatenate(
            [all_tok[r].reshape(-1, features) for r in lanes_a + lanes_b]
            + [tok_rows.astype(bf16)],
            axis=0,
        )
        cot = jnp.concatenate(
            [
                jnp.concatenate([main_of(j) for j in range(blocks)], axis=1).astype(f32),
                cot_rows,
            ],
            axis=0,
        )
        og_ref[rows, :] = (w * cot).astype(bf16)
        t = t_ref[rows, :]
        gate_pre = jnp.dot(t, wg[...], preferred_element_type=f32)
        up_proj = jnp.dot(t, wu[...], preferred_element_type=f32)
        hidden_grad = lax.dot_general(og_ref[rows, :], wd[...], NT, preferred_element_type=f32)
        sig = jax.nn.sigmoid(gate_pre)
        act = gate_pre * sig
        h_ref[rows, :] = (act * up_proj).astype(bf16)
        gg_ref[rows, :] = (hidden_grad * up_proj * sig * (1.0 + gate_pre * (1.0 - sig))).astype(
            bf16
        )
        ug_ref[rows, :] = (hidden_grad * act).astype(bf16)

    main_rows = experts * TILE
    group_rows = main_rows + levels * 8
    early = (all_t, all_og, all_h, all_gg, all_ug)
    late = (late_t, late_og, late_h, late_gg, late_ug)

    column(1)
    beside(0)
    column(2)
    beside(1)
    column(3)
    from_pair(OWN, slot(d, 0, pc), levels)
    for copy in weight_copies:
        copy.wait()
    group([(d, 0, levels)], early + (0,))
    beside(2)
    own = pl.ds(0, group_rows)
    rg = lax.dot_general(all_gg[own, :], wg[...], NT, preferred_element_type=f32)
    rg = rg + lax.dot_general(all_ug[own, :], wu[...], NT, preferred_element_type=f32)
    lane_rows = main_rows // 2
    for j in range(blocks):
        cols = slice(j * LANES, (j + 1) * LANES)
        for core in range(2):
            row_out[core, :, j] = (
                rg[core * lane_rows : (core + 1) * lane_rows, cols]
                .reshape(levels, TILE, LANES)
                .astype(bf16)
            )
    for j in range(half):
        lo = rg[main_rows:, j * LANES : (j + 1) * LANES].reshape(levels, 8, LANES)
        hi = rg[main_rows:, (half + j) * LANES : (half + j + 1) * LANES].reshape(levels, 8, LANES)
        both = jnp.concatenate([lo, hi], axis=1).astype(bf16)
        for core in range(2):
            row_out[core, :, blocks + j] = both

    def row_copy(f):
        src, dst = row_out.at[pc], pair_in
        if not f:
            src, dst = row_out.at[pc, :, pl.ds(0, blocks)], pair_in.at[:, pl.ds(0, blocks)]
        return remote(src, dst, row_sem.at[0], row_sem.at[1], at_pair)

    either(hot, lambda f: row_copy(f).start())
    across(0)
    from_pair(NEAR, 0, levels)
    group([(dx, near, 2), (dy, near, 2)], early + (group_rows,))

    either(hot, lambda f: row_copy(f).wait_recv())
    for level in range(levels):
        row_sum[level, :blocks] = (
            row_out[c, level, :blocks].astype(f32) + pair_in[level, :blocks].astype(f32)
        ).astype(bf16)

    @pl.when(hot)
    def _():
        for level in range(levels):
            row_sum[level, blocks:] = (
                row_out[c, level, blocks:].astype(f32) + pair_in[level, blocks:].astype(f32)
            ).astype(bf16)

    def z_copy(level, sender, send, peer, f):
        src, dst = row_sum.at[level], z_in.at[sender]
        if not f:
            part = pl.ds(0, blocks)
            src, dst = row_sum.at[level, part], z_in.at[sender, part]
        return remote(src, dst, z_send.at[send], z_recv.at[sender], peer)

    for level in range(levels):

        @pl.when(z != level)
        def _():
            either(hot, lambda f: z_copy(level, z, level, (d, level * 2 + c), f).start())

    across(1)
    beside(3)
    from_pair(DD_NEAR, 0, 2)
    group([(dd, near, 2)], early + (2 * group_rows,))
    from_pair(FAR, 0, levels)
    group([(dx, far, 2), (dy, far, 2)], late + (0,))
    across(2)
    across(3)

    share = features // 4
    cols = pl.ds(pl.multiple_of(d * share, LANES), share)
    t_cols = all_t[:, cols]
    acc_gate[...] = lax.dot_general(t_cols, all_gg[...], TN, preferred_element_type=f32)
    acc_up[...] = lax.dot_general(t_cols, all_ug[...], TN, preferred_element_type=f32)
    acc_down[...] = lax.dot_general(all_h[...], all_og[...], TN, preferred_element_type=f32)
    z_in[z] = row_sum[z]

    from_pair(DD_FAR, 0, 2)
    group([(dd, far, 2)], late + (group_rows,))
    late_cols[...] = late_t[:, cols]

    for level in range(levels):

        @pl.when(z != level)
        def _():
            z_copy(level, level, level, at_pair, level < hot_levels).wait_recv()

    total = z_in[0, :blocks].astype(f32)
    spilled = z_in[0, blocks:].astype(f32)
    for level in range(1, levels):
        total = total + z_in[level, :blocks].astype(f32)
        if level < hot_levels:
            spilled = spilled + z_in[level, blocks:].astype(f32)
    kept_row = lax.broadcasted_iota(jnp.int32, (8, LANES), 0) < 4
    blank = jnp.zeros((8, LANES), f32)
    for j in range(blocks):
        tg_ref[:TILE, j * LANES : (j + 1) * LANES] = total[j].astype(bf16)
    for j in range(half):
        for at, rows in ((j, spilled[j][:8]), (half + j, spilled[j][8:])):
            rows = jnp.where(c == 0, rows, pltpu.roll(rows, 4, 0))
            tg_ref[TILE:, at * LANES : (at + 1) * LANES] = jnp.concatenate(
                [jnp.where(kept_row, rows, 0.0), blank], axis=0
            ).astype(bf16)

    def sent(send, p, count, f):
        region = pl.ds(0, count)
        part = all_tok.at[region]
        if p == 1:
            part = slab.at[region] if f else slab.at[region, pl.ds(0, spill_at)]
        remote(part, part, send, recv_sem.at[0, 0], at_x).wait_send()

    for p in range(2):
        for way in (X, Y):
            send = flat_send.at[way, p]
            more = (p + c) % 2 == (1 if way == X else 0)
            less = (p + c) % 2 == (0 if way == X else 1)
            wide = True if p == 0 else hot
            pl.when(less)(lambda: either(wide, lambda f: sent(send, p, levels, f)))
            pl.when(more)(lambda: either(wide, lambda f: sent(send, p, 2 * levels, f)))
        either(wide, lambda f: sent(flat_send.at[PAIR, p], p, 4 * levels, f))
        for level in range(1, levels):
            pl.when(jnp.logical_and(level >= z, low_z))(
                lambda: sent(down_send.at[p, level - 1], p, 1, True)
            )
        for level in range(levels - 1):
            pl.when(jnp.logical_and(level <= z, up_z))(
                lambda: either(
                    True if p == 0 else z + 1 < hot_levels,
                    lambda f: sent(up_send.at[p, level], p, 1, f),
                )
            )
    either(hot, lambda f: row_copy(f).wait_send())
    for level in range(levels):

        @pl.when(z != level)
        def _():
            either(hot, lambda f: z_copy(level, z, level, at_pair, f).wait_send())


def finish_kernel(
    tg_ref,
    acc_gate,
    acc_up,
    acc_down,
    late_cols,
    late_og,
    late_h,
    late_gg,
    late_ug,
    tg_out,
    gg_out,
    gu_out,
    gd_out,
    gg_ref,
    gu_ref,
    gd_ref,
    sem,
):
    bf16, f32 = jnp.bfloat16, jnp.float32
    copies = [pltpu.make_async_copy(tg_ref, tg_out, sem.at[0])]
    copies[0].start()
    hidden_size = acc_gate.shape[1]

    def write(src, dst):
        copies.append(pltpu.make_async_copy(src, dst, sem.at[len(copies)]))
        copies[-1].start()

    for j in range(hidden_size // LANES):
        rows = pl.ds(j * LANES, LANES)
        term = lax.dot_general(late_h[:, rows], late_og[...], TN, preferred_element_type=f32)
        gd_ref[rows, :] = (acc_down[rows, :] + term).astype(bf16)
        write(gd_ref.at[rows], gd_out.at[0, rows])
    term = lax.dot_general(late_cols[...], late_gg[...], TN, preferred_element_type=f32)
    gg_ref[...] = (acc_gate[...] + term).astype(bf16)
    write(gg_ref, gg_out.at[0])
    term = lax.dot_general(late_cols[...], late_ug[...], TN, preferred_element_type=f32)
    gu_ref[...] = (acc_up[...] + term).astype(bf16)
    write(gu_ref, gu_out.at[0])
    for copy in copies:
        copy.wait()


def dense_shards(tokens, cotangent, routes, combine, hot_experts, extra_slots, w_gate, w_up, w_down):
    experts = lax.axis_size("expert")
    replicas = lax.axis_size("dp")
    token_count, features = tokens.shape
    hidden_size = w_gate.shape[2]
    blocks = features // LANES
    half = blocks // 2
    levels = experts // 2
    slots = replicas * experts
    share = features // replicas
    group_rows = experts * TILE + levels * 8
    early_rows, late_rows = 2 * group_rows + group_rows // 2, group_rows + group_rows // 2
    bf16, f32 = jnp.bfloat16, jnp.float32
    vmem = pl.BlockSpec(memory_space=pltpu.VMEM)
    hbm = pl.BlockSpec(memory_space=pltpu.HBM)
    dma = pltpu.SemaphoreType.DMA
    operands = [
        pltpu.with_memory_space_constraint(a, pltpu.HBM)
        for a in (
            tokens,
            cotangent,
            routes.T,
            combine.T,
            hot_experts,
            extra_slots,
            w_gate,
            w_up,
            w_down,
        )
    ]
    parts = pl.pallas_call(
        functools.partial(dense_kernel, experts),
        out_shape=(
            jax.ShapeDtypeStruct((token_count, features), bf16),
            jax.ShapeDtypeStruct((share, hidden_size), f32),
            jax.ShapeDtypeStruct((share, hidden_size), f32),
            jax.ShapeDtypeStruct((hidden_size, features), f32),
            jax.ShapeDtypeStruct((late_rows, share), bf16),
            jax.ShapeDtypeStruct((late_rows, features), bf16),
            jax.ShapeDtypeStruct((late_rows, hidden_size), bf16),
            jax.ShapeDtypeStruct((late_rows, hidden_size), bf16),
            jax.ShapeDtypeStruct((late_rows, hidden_size), bf16),
        ),
        in_specs=[hbm] * 9,
        out_specs=(vmem,) * 9,
        scratch_shapes=[
            pltpu.VMEM((TILE, features), bf16),
            pltpu.VMEM(cotangent.shape, bf16),
            pltpu.VMEM(routes.shape[::-1], jnp.int32),
            pltpu.VMEM(routes.shape[::-1], bf16),
            pltpu.SMEM(hot_experts.shape, jnp.int32),
            pltpu.SMEM(hot_experts.shape, jnp.int32),
            pltpu.VMEM((slots, TILE, features), bf16),
            pltpu.VMEM((slots, blocks + 1 + half, TILE, LANES), bf16),
            pltpu.VMEM((features, hidden_size), bf16),
            pltpu.VMEM((features, hidden_size), bf16),
            pltpu.VMEM((hidden_size, features), bf16),
            pltpu.VMEM((early_rows, features), bf16),
            pltpu.VMEM((early_rows, features), bf16),
            pltpu.VMEM((early_rows, hidden_size), bf16),
            pltpu.VMEM((early_rows, hidden_size), bf16),
            pltpu.VMEM((early_rows, hidden_size), bf16),
            pltpu.VMEM((late_rows, features), bf16),
            pltpu.VMEM((2, levels, blocks + half, TILE, LANES), bf16),
            pltpu.VMEM((levels, blocks + half, TILE, LANES), bf16),
            pltpu.VMEM((levels, blocks + half, TILE, LANES), bf16),
            pltpu.VMEM((levels, blocks + half, TILE, LANES), bf16),
            dma((7,)),
            dma((3,)),
            dma((3, 2)),
            dma((2, levels - 1)),
            dma((2, levels - 1)),
            dma((2, slots // 2)),
            dma((2, 5)),
            dma((2,)),
            dma((levels,)),
            dma((levels,)),
            pltpu.SemaphoreType.REGULAR((3,)),
        ],
        compiler_params=pltpu.CompilerParams(
            collective_id=0, has_side_effects=True, vmem_limit_bytes=32 * 1024 * 1024
        ),
    )(*operands)
    return pl.pallas_call(
        finish_kernel,
        out_shape=(
            jax.ShapeDtypeStruct((token_count, features), bf16),
            jax.ShapeDtypeStruct((1, share, hidden_size), bf16),
            jax.ShapeDtypeStruct((1, share, hidden_size), bf16),
            jax.ShapeDtypeStruct((1, hidden_size, features), bf16),
        ),
        in_specs=[vmem] * len(parts),
        out_specs=(hbm,) * 4,
        scratch_shapes=[
            pltpu.VMEM((share, hidden_size), bf16),
            pltpu.VMEM((share, hidden_size), bf16),
            pltpu.VMEM((hidden_size, features), bf16),
            dma((3 + hidden_size // LANES,)),
        ],
        compiler_params=pltpu.CompilerParams(vmem_limit_bytes=16 * 1024 * 1024),
    )(*parts)


def solution(mesh):
    in_specs = (
        P(("dp", "expert"), None),
        P(("dp", "expert"), None),
        P(("dp", "expert"), None),
        P(("dp", "expert"), None),
        P(),
        P(),
        P("expert", None, None),
        P("expert", None, None),
        P("expert", None, None),
    )
    out_specs = (
        P(("dp", "expert"), None),
        P("expert", "dp", None),
        P("expert", "dp", None),
        P("expert", None, None),
    )

    def body(*args):
        token_count, features = args[0].shape
        if dense_fits(dict(mesh.shape), token_count, features, args[2].shape[1], args[6].shape[2]):
            return dense_shards(*args)
        return shards(*args)

    return jax.shard_map(body, mesh=mesh, in_specs=in_specs, out_specs=out_specs, check_vma=False)
```

time: 30.1 us -> 26.2 us (0.87)
  Pallas kernels: 29.3 us -> 25.4 us
    pallas_call x1, Pallas kernels: 28.2 us -> 24.1 us  [dense_shards(): pl.pallas_call(functools.partial(dense_kernel, experts), out_shape=(jax.S...]
where the time goes in v2:
time: 26.2 us; the launch traced here: 26.1 us
  Pallas kernels  25.4 us (97%)
  between operations  0.64 us (2%)
    pallas_call x1, Pallas kernels, dense_shards(): pl.pallas_call(functools.partial(dense_kernel, experts), out_shape=(jax.S...  24.1 us
    pallas_call x1, Pallas kernels, dense_shards(): pl.pallas_call(finish_kernel, out_shape=(jax.ShapeDtypeStruct((token_coun...  1.33 us

profile of v2, /device:TPU:0, one launch (start us, length us, event | category | flops | bytes accessed | tf_op | source)
XLA Modules:
  0.0 26.1 jit_solution(4365729194043627943)
XLA Ops:
  0.6 24.1 %shard_map.120 = (bf16[32,1024]{1,0:T(8,128)(2,1)S(1)}, f32[256,384]{1,0:T(8,128)S(1)}, f32[256,384]{1,0:T(8,128)S(1)}, f32[384,1024]{1,0:T(8,128)S(1)}, bf16[24...) custom-call(bf16[32,1024]{1,0:T(8,128)(2,1)} %tok_hbm.1, ...), custom_call_target="tpu_custom_call" | custom-call | tf_op jit(solution)/shard_map/pallas_call | solution.py:751
  24.7 1.3 %shard_map.121 = (bf16[32,1024]{1,0:T(8,128)(2,1)}, bf16[1,256,384]{2,1,0:T(8,128)(2,1)}, bf16[1,256,384]{2,1,0:T(8,128)(2,1)}, bf16[1,384,1024]{2,1,0:T(8,128)(2,1)}) custom-call(bf16[32,1024]{1,0:T(8,128)(2,1)S(1)} %get-tuple-element.13.tg_ref, f32[256,384]{1,0:T(8,128)S(1)} %get-tuple-element.14.acc_gate, f32[256,384]{1,0:T(8,128)S(1)} %get-tuple-element.15.acc_up, ...), custom_call_target="tpu_custom_call" | custom-call | tf_op jit(solution)/shard_map/pallas_call | solution.py:804

commit v3 on v2

--- a/solution.py
+++ b/solution.py
@@ -180,8 +180,9 @@
     in_sem,
     w_sem,
     flat_send,
-    down_send,
-    up_send,
+    own_send,
+    z_own,
+    diag_send,
     recv_sem,
     pair_recv,
     row_sem,
@@ -209,8 +210,13 @@
     hot = z < hot_levels
     low_x, low_y, low_z = d % 2 == 1, d // 2 == 1, z > 0
     up_x, up_y, up_z = d % 2 == 0, d // 2 == 0, z < levels - 1
+    first_z, last_z = z == 0, z == levels - 1
+    at_below, at_above = (d, jnp.maximum(e - 2, 0)), (d, jnp.minimum(e + 2, experts - 1))
+    at_top, at_bottom = (d, (levels - 1) * 2 + c), (d, c)
     at_x, at_y, at_pair = (dx, e), (dy, e), (d, z * 2 + pc)
-    at_below, at_above = (d, jnp.maximum(e - 2, 0)), (d, jnp.minimum(e + 2, experts - 1))
+    at_diag = (dd, e)
+    upper = z >= hot_levels
+    low_d, up_d = jnp.logical_and(upper, d > dd), jnp.logical_and(upper, d < dd)
 
     def slot(dp, level, core):
         return (dp * 2 + core) * levels + level
@@ -245,6 +251,8 @@
     pl.when(up_x)(lambda: greet(at_x))
     pl.when(up_y)(lambda: greet(at_y))
     pl.when(up_z)(lambda: greet(at_above))
+    pl.when(first_z)(lambda: greet(at_top))
+    pl.when(up_d)(lambda: greet(at_diag))
     for copy in input_copies + [own_tokens] + weight_copies:
         copy.start()
 
@@ -282,17 +290,44 @@
 
     X, Y, PAIR = range(3)
 
+    def to_side(way, dp, level, p, full, own):
+        peer = at_x if way == X else at_y
+        send = flat_send.at[way, p]
+        if p == 0 or not own:
+            push(dp, level, p, full, send, peer, own)
+            return
+        pl.when(hot)(lambda: push(dp, level, p, True, send, peer, own))
+        pl.when(upper)(lambda: push(dp, level, p, True, own_send.at[way], peer, own))
+
     def to_x(dp, level, p, own=False):
-        push(dp, level, p, hot, flat_send.at[X, p], at_x, own)
+        to_side(X, dp, level, p, True if own else hot, own)
 
     def to_y(dp, level, p, own=False):
-        push(dp, level, p, hot, flat_send.at[Y, p], at_y, own)
-
-    def to_above(level, p, own=False):
-        push(d, level, p, z + 1 < hot_levels, up_send.at[p, level], at_above, own)
-
-    def to_below(level, p, own=False):
-        push(d, level, p, True, down_send.at[p, level - 1], at_below, own)
+        to_side(Y, dp, level, p, True if own else hot, own)
+
+    def to_below(p):
+        push(d, z, p, True, z_own.at[p, 0], at_below, True)
+
+    def to_above(p):
+        push(d, z, p, z + 1 < hot_levels, z_own.at[p, 1], at_above, True)
+
+    def to_top(p):
+        push(d, z, p, False, z_own.at[p, 0], at_top, True)
+
+    def to_bottom(p):
+        push(d, z, p, True, z_own.at[p, 2], at_bottom, True)
+
+    def pass_down(level, p, at):
+        push(d, level, p, True, z_own.at[p, at], at_below)
+
+    def pass_up(level, p):
+        push(d, level, p, False, z_own.at[p, 3], at_above)
+
+    def to_diag(p):
+        push(d, z, p, True, diag_send.at[p, 0], at_diag, True)
+
+    def pass_across(p, at, peer):
+        push(dd, z, p, True, diag_send.at[p, at], peer)
 
     def to_pair(dp, level, p, bank, own=False):
         s = slot(dp, level, c)
@@ -304,7 +339,7 @@
 
         either(True if p == 0 else hot, go)
 
-    def arrived(dp, level, p, above=False):
+    def arrived(dp, level, p, full):
         s = slot(dp, level, c)
 
         def go(f):
@@ -312,23 +347,29 @@
             at = recv_sem.at[p, dp * levels + level]
             remote(dst, dst, flat_send.at[X, p], at, at_x).wait_recv()
 
-        either(True if p == 0 or above else hot, go)
-
-    pl.semaphore_wait(barrier, 1 + d % 2 + d // 2 + jnp.minimum(z, 1))
+        either(True if p == 0 else full, go)
+
+    pl.semaphore_wait(
+        barrier, 1 + d % 2 + d // 2 + jnp.minimum(z, 1) + z // (levels - 1) + upper_half * (d // 2)
+    )
 
     def tell(way, peer):
         pl.semaphore_signal(ready.at[way], inc=1, device_id=peer, device_id_type=MESH)
 
     pl.when(low_x)(lambda: tell(0, at_x))
     pl.when(low_y)(lambda: tell(1, at_y))
-    pl.when(low_z)(lambda: tell(2, at_below))
-
-    OWN, NEAR, FAR, DD_NEAR, DD_FAR = range(5)
+    pl.when(low_z)(lambda: tell(3, at_below))
+    pl.when(last_z)(lambda: tell(4, at_bottom))
+    pl.when(low_d)(lambda: tell(2, at_diag))
+
+    OWN, NEAR, FAR, DD = range(4)
 
     def to_lower(p):
-        pl.when(low_z)(lambda: to_below(z, p, True))
+        pl.when(low_z)(lambda: to_below(p))
+        pl.when(last_z)(lambda: to_bottom(p))
         pl.when(low_x)(lambda: to_x(d, z, p, True))
         pl.when(low_y)(lambda: to_y(d, z, p, True))
+        pl.when(low_d)(lambda: to_diag(p))
         to_pair(d, z, p, OWN, True)
 
     to_lower(0)
@@ -376,58 +417,66 @@
             for p in range(2):
                 act(p)
 
-    to_upper(2, up_z, lambda p: to_above(z, p, True))
+    to_upper(3, up_z, to_above)
     to_upper(0, up_x, lambda p: to_x(d, z, p, True))
     to_upper(1, up_y, lambda p: to_y(d, z, p, True))
+    to_upper(2, up_d, to_diag)
     own_tokens.wait()
 
     def at_distance(dist, visit):
         if dist == 0:
             visit(z, 0)
             return
+        pl.when(z - dist >= 0)(lambda: visit(z - dist, -1))
         pl.when(z + dist < levels)(lambda: visit(z + dist, 1))
-        pl.when(z - dist >= 0)(lambda: visit(z - dist, -1))
 
     def bank_of(level):
         return (level // 2 + upper_half) % 2
 
-    def column(dist):
-        for p in range(2):
-
-            def visit(level, side):
-                arrived(d, level, p, side > 0)
-                if side > 0:
-                    pl.when(low_z)(lambda: to_below(level, p))
-                else:
-                    pl.when(up_z)(lambda: to_above(level, p))
-                to_x(d, level, p)
-                to_y(d, level, p)
-                to_pair(d, level, p, OWN)
-
-            at_distance(dist, visit)
-
-    def beside(dist):
-        for p in range(2):
-
-            def visit(level, side):
-                bank = NEAR + bank_of(level)
-                arrived(dx, level, p)
-                pl.when((p + c) % 2 == 0)(lambda: to_y(dx, level, p))
-                to_pair(dx, level, p, bank)
-                arrived(dy, level, p)
-                pl.when((p + c) % 2 == 1)(lambda: to_x(dy, level, p))
-                to_pair(dy, level, p, bank)
-
-            at_distance(dist, visit)
-
-    def across(dist):
-        for p in range(2):
-
-            def visit(level, side):
-                arrived(dd, level, p)
-                to_pair(dd, level, p, DD_NEAR + bank_of(level))
-
-            at_distance(dist, visit)
+    def column(dist, p):
+        def visit(level, side):
+            arrived(d, level, p, True if side > 0 else hot)
+            if dist == 1 and side > 0:
+                pl.when(low_z)(lambda: pass_down(level, p, 2))
+            elif dist == 1:
+                pl.when(up_z)(lambda: pass_up(level, p))
+            to_x(d, level, p)
+            to_y(d, level, p)
+            to_pair(d, level, p, OWN)
+
+        at_distance(dist, visit)
+
+    def beside(dist, p):
+        full = True if dist == 0 else hot
+        keep = (hot, True, low_z, low_z)[dist]
+
+        def visit(level, side, keep=keep):
+            bank = NEAR + bank_of(level)
+            if dist == 1 and side < 0:
+                keep = z != 1
+            arrived(dx, level, p, full)
+            turn = jnp.logical_and((p + c) % 2 == 0, keep)
+            pl.when(turn)(lambda: to_y(dx, level, p))
+            to_pair(dx, level, p, bank)
+            arrived(dy, level, p, full)
+            turn = jnp.logical_and((p + c) % 2 == 1, keep)
+            pl.when(turn)(lambda: to_x(dy, level, p))
+            to_pair(dy, level, p, bank)
+
+        at_distance(dist, visit)
+
+    def across(dist, p):
+        full = True if dist == 0 else hot
+
+        def visit(level, side):
+            arrived(dd, level, p, full)
+            if dist == 0:
+                pl.when(last_z)(lambda: pass_across(p, 1, at_bottom))
+                pl.when(z == 2)(lambda: pass_across(p, 1, at_bottom))
+                pl.when(first_z)(lambda: pass_across(p, 1, at_above))
+            to_pair(dd, level, p, DD)
+
+        at_distance(dist, visit)
 
     def from_pair(bank, at, count):
         region = pl.ds(at, count)
@@ -530,16 +579,29 @@
     early = (all_t, all_og, all_h, all_gg, all_ug)
     late = (late_t, late_og, late_h, late_gg, late_ug)
 
-    column(1)
-    beside(0)
-    column(2)
-    beside(1)
-    column(3)
+    for p in range(2):
+        beside(0, p)
+        column(1, p)
+    to_upper(4, first_z, to_top)
+
+    for p in range(2):
+        for dist in (2, 3):
+            column(dist, p)
+
+    @pl.when(upper)
+    def _():
+        for p in range(2):
+            across(0, p)
+
     from_pair(OWN, slot(d, 0, pc), levels)
     for copy in weight_copies:
         copy.wait()
     group([(d, 0, levels)], early + (0,))
-    beside(2)
+    @pl.when(hot)
+    def _():
+        for p in range(2):
+            across(0, p)
+
     own = pl.ds(0, group_rows)
     rg = lax.dot_general(all_gg[own, :], wg[...], NT, preferred_element_type=f32)
     rg = rg + lax.dot_general(all_ug[own, :], wu[...], NT, preferred_element_type=f32)
@@ -566,9 +628,8 @@
         return remote(src, dst, row_sem.at[0], row_sem.at[1], at_pair)
 
     either(hot, lambda f: row_copy(f).start())
-    across(0)
-    from_pair(NEAR, 0, levels)
-    group([(dx, near, 2), (dy, near, 2)], early + (group_rows,))
+    for p in range(2):
+        beside(1, p)
 
     either(hot, lambda f: row_copy(f).wait_recv())
     for level in range(levels):
@@ -596,26 +657,45 @@
         def _():
             either(hot, lambda f: z_copy(level, z, level, (d, level * 2 + c), f).start())
 
-    across(1)
-    beside(3)
-    from_pair(DD_NEAR, 0, 2)
-    group([(dd, near, 2)], early + (2 * group_rows,))
-    from_pair(FAR, 0, levels)
-    group([(dx, far, 2), (dy, far, 2)], late + (0,))
-    across(2)
-    across(3)
-
+    @pl.when(low_z)
+    def _():
+        for dist in (2, 3):
+            for p in range(2):
+                beside(dist, p)
+
+    from_pair(NEAR, 0, levels)
+    group([(dx, near, 2), (dy, near, 2)], early + (group_rows,))
+
+    @pl.when(first_z)
+    def _():
+        for dist in (2, 3):
+            for p in range(2):
+                beside(dist, p)
+
+    def across_when(cond, *dists):
+        @pl.when(cond)
+        def _():
+            for dist in dists:
+                for p in range(2):
+                    across(dist, p)
+
+    across_when(first_z, 3, 2)
+    across_when(low_z, 1)
+    across_when(last_z, 2, 3)
     share = features // 4
     cols = pl.ds(pl.multiple_of(d * share, LANES), share)
     t_cols = all_t[:, cols]
     acc_gate[...] = lax.dot_general(t_cols, all_gg[...], TN, preferred_element_type=f32)
     acc_up[...] = lax.dot_general(t_cols, all_ug[...], TN, preferred_element_type=f32)
     acc_down[...] = lax.dot_general(all_h[...], all_og[...], TN, preferred_element_type=f32)
+    from_pair(FAR, 0, levels)
+    group([(dx, far, 2), (dy, far, 2)], late + (0,))
+    across_when(first_z, 1)
+    across_when(jnp.logical_and(low_z, up_z), 2)
+    from_pair(DD, 0, levels)
+    group([(dd, 0, levels)], late + (group_rows,))
+    late_cols[...] = late_t[:, cols]
     z_in[z] = row_sum[z]
-
-    from_pair(DD_FAR, 0, 2)
-    group([(dd, far, 2)], late + (group_rows,))
-    late_cols[...] = late_t[:, cols]
 
     for level in range(levels):
 
@@ -640,33 +720,46 @@
                 [jnp.where(kept_row, rows, 0.0), blank], axis=0
             ).astype(bf16)
 
-    def sent(send, p, count, f):
-        region = pl.ds(0, count)
+    def sent(send, p, count, f, first=0):
+        region = pl.ds(first, count)
         part = all_tok.at[region]
         if p == 1:
             part = slab.at[region] if f else slab.at[region, pl.ds(0, spill_at)]
         remote(part, part, send, recv_sem.at[0, 0], at_x).wait_send()
 
     for p in range(2):
+        wide = True if p == 0 else hot
         for way in (X, Y):
             send = flat_send.at[way, p]
             more = (p + c) % 2 == (1 if way == X else 0)
             less = (p + c) % 2 == (0 if way == X else 1)
-            wide = True if p == 0 else hot
-            pl.when(less)(lambda: either(wide, lambda f: sent(send, p, levels, f)))
-            pl.when(more)(lambda: either(wide, lambda f: sent(send, p, 2 * levels, f)))
+            for at, extra in ((0, 2), (1, levels - 1), (2, levels - 1)):
+                here = (z == 0, z == 1, upper)[at]
+                own = 1 if at == 2 and p == 1 else 0
+                f = not (at == 2 and p == 1)
+                pl.when(jnp.logical_and(here, less))(
+                    functools.partial(sent, send, p, levels - own, f)
+                )
+                pl.when(jnp.logical_and(here, more))(
+                    functools.partial(sent, send, p, levels - own + extra, f)
+                )
+            if p == 1:
+                pl.when(upper)(functools.partial(sent, own_send.at[way], 1, 1, True))
         either(wide, lambda f: sent(flat_send.at[PAIR, p], p, 4 * levels, f))
-        for level in range(1, levels):
-            pl.when(jnp.logical_and(level >= z, low_z))(
-                lambda: sent(down_send.at[p, level - 1], p, 1, True)
-            )
-        for level in range(levels - 1):
-            pl.when(jnp.logical_and(level <= z, up_z))(
-                lambda: either(
-                    True if p == 0 else z + 1 < hot_levels,
-                    lambda f: sent(up_send.at[p, level], p, 1, f),
-                )
-            )
+
+        pl.when(upper)(functools.partial(sent, diag_send.at[p, 0], p, 1, True))
+        pl.when(z != 1)(functools.partial(sent, diag_send.at[p, 1], p, 1, True))
+
+        pl.when(first_z)(functools.partial(sent, z_own.at[p, 0], p, 1, False))
+        pl.when(first_z)(functools.partial(sent, z_own.at[p, 1], p, 1, True))
+        pl.when(low_z)(functools.partial(sent, z_own.at[p, 0], p, 1, True))
+        pl.when(low_z)(functools.partial(sent, z_own.at[p, 2], p, 1, True))
+
+        @pl.when(jnp.logical_and(low_z, up_z))
+        def _():
+            sent(z_own.at[p, 1], p, 1, False)
+            sent(z_own.at[p, 3], p, 1, False)
+
     either(hot, lambda f: row_copy(f).wait_send())
     for level in range(levels):
 
@@ -729,7 +822,7 @@
     slots = replicas * experts
     share = features // replicas
     group_rows = experts * TILE + levels * 8
-    early_rows, late_rows = 2 * group_rows + group_rows // 2, group_rows + group_rows // 2
+    early_rows, late_rows = 2 * group_rows, 2 * group_rows
     bf16, f32 = jnp.bfloat16, jnp.float32
     vmem = pl.BlockSpec(memory_space=pltpu.VMEM)
     hbm = pl.BlockSpec(memory_space=pltpu.HBM)
@@ -788,14 +881,15 @@
             dma((7,)),
             dma((3,)),
             dma((3, 2)),
-            dma((2, levels - 1)),
-            dma((2, levels - 1)),
+            dma((2,)),
+            dma((2, levels)),
+            dma((2, 2)),
             dma((2, slots // 2)),
-            dma((2, 5)),
+            dma((2, 4)),
             dma((2,)),
             dma((levels,)),
             dma((levels,)),
-            pltpu.SemaphoreType.REGULAR((3,)),
+            pltpu.SemaphoreType.REGULAR((5,)),
         ],
         compiler_params=pltpu.CompilerParams(
             collective_id=0, has_side_effects=True, vmem_limit_bytes=32 * 1024 * 1024

time: 26.2 us -> 25.4 us (0.969)
  the two profiles are of different devices: /device:TPU:0 before, /device:TPU:9 now
where the time goes in v3:
time: 25.4 us; the launch traced here: 25.2 us
  Pallas kernels  24.6 us (97%)
  between operations  0.64 us (3%)
    pallas_call x1, Pallas kernels, dense_shards(): pl.pallas_call(functools.partial(dense_kernel, experts), out_shape=(jax.S...  23 us
    pallas_call x1, Pallas kernels, dense_shards(): pl.pallas_call(finish_kernel, out_shape=(jax.ShapeDtypeStruct((token_coun...  1.58 us

profile of v3, /device:TPU:9, one launch (start us, length us, event | category | flops | bytes accessed | tf_op | source)
XLA Modules:
  0.0 25.2 jit_solution(16680493617573186552)
XLA Ops:
  0.6 23.0 %shard_map.120 = (bf16[32,1024]{1,0:T(8,128)(2,1)S(1)}, f32[256,384]{1,0:T(8,128)S(1)}, f32[256,384]{1,0:T(8,128)S(1)}, f32[384,1024]{1,0:T(8,128)S(1)}, bf16[32...) custom-call(bf16[32,1024]{1,0:T(8,128)(2,1)} %tok_hbm.1, ...), custom_call_target="tpu_custom_call" | custom-call | tf_op jit(solution)/shard_map/pallas_call | solution.py:844
  23.6 1.6 %shard_map.121 = (bf16[32,1024]{1,0:T(8,128)(2,1)}, bf16[1,256,384]{2,1,0:T(8,128)(2,1)}, bf16[1,256,384]{2,1,0:T(8,128)(2,1)}, bf16[1,384,1024]{2,1,0:T(8,128)(2,1)}) custom-call(bf16[32,1024]{1,0:T(8,128)(2,1)S(1)} %get-tuple-element.13.tg_ref, f32[256,384]{1,0:T(8,128)S(1)} %get-tuple-element.14.acc_gate, f32[256,384]{1,0:T(8,128)S(1)} %get-tuple-element.15.acc_up, ...), custom_call_target="tpu_custom_call" | custom-call | tf_op jit(solution)/shard_map/pallas_call | solution.py:898

commit v4 on v3

--- a/solution.py
+++ b/solution.py
@@ -173,20 +173,21 @@
     all_gg,
     all_ug,
     late_t,
+    mid_t,
+    mid_og,
+    mid_h,
+    mid_gg,
+    mid_ug,
     row_out,
     pair_in,
     row_sum,
     z_in,
     in_sem,
     w_sem,
-    flat_send,
-    own_send,
-    z_own,
-    diag_send,
+    send_sem,
     recv_sem,
     pair_recv,
     row_sem,
-    z_send,
     z_recv,
     ready,
 ):
@@ -247,7 +248,7 @@
     def greet(peer):
         pl.semaphore_signal(barrier, inc=1, device_id=peer, device_id_type=MESH)
 
-    greet(at_pair)
+    pl.when(c == 0)(lambda: greet(at_pair))
     pl.when(up_x)(lambda: greet(at_x))
     pl.when(up_y)(lambda: greet(at_y))
     pl.when(up_z)(lambda: greet(at_above))
@@ -278,56 +279,48 @@
             device_id_type=MESH,
         )
 
-    def push(dp, level, p, full, send, peer, own=False):
+    def kind(p, f):
+        return send_sem.at[0 if p == 0 else 1 if f else 2]
+
+    def push(dp, level, p, full, peer, own=False):
         s = slot(dp, level, c)
 
         def go(f):
             dst = piece(s, p, f)
             src = tok_hbm.at[pl.ds(0, TILE)] if own and p == 0 else dst
-            remote(src, dst, send, recv_sem.at[p, dp * levels + level], peer).start()
+            remote(src, dst, kind(p, f), recv_sem.at[p, dp * levels + level], peer).start()
 
         either(True if p == 0 else full, go)
 
-    X, Y, PAIR = range(3)
-
-    def to_side(way, dp, level, p, full, own):
-        peer = at_x if way == X else at_y
-        send = flat_send.at[way, p]
-        if p == 0 or not own:
-            push(dp, level, p, full, send, peer, own)
-            return
-        pl.when(hot)(lambda: push(dp, level, p, True, send, peer, own))
-        pl.when(upper)(lambda: push(dp, level, p, True, own_send.at[way], peer, own))
-
     def to_x(dp, level, p, own=False):
-        to_side(X, dp, level, p, True if own else hot, own)
+        push(dp, level, p, True if own else hot, at_x, own)
 
     def to_y(dp, level, p, own=False):
-        to_side(Y, dp, level, p, True if own else hot, own)
+        push(dp, level, p, True if own else hot, at_y, own)
 
     def to_below(p):
-        push(d, z, p, True, z_own.at[p, 0], at_below, True)
+        push(d, z, p, True, at_below, True)
 
     def to_above(p):
-        push(d, z, p, z + 1 < hot_levels, z_own.at[p, 1], at_above, True)
+        push(d, z, p, z + 1 < hot_levels, at_above, True)
 
     def to_top(p):
-        push(d, z, p, False, z_own.at[p, 0], at_top, True)
+        push(d, z, p, False, at_top, True)
 
     def to_bottom(p):
-        push(d, z, p, True, z_own.at[p, 2], at_bottom, True)
-
-    def pass_down(level, p, at):
-        push(d, level, p, True, z_own.at[p, at], at_below)
+        push(d, z, p, True, at_bottom, True)
+
+    def pass_down(level, p):
+        push(d, level, p, True, at_below)
 
     def pass_up(level, p):
-        push(d, level, p, False, z_own.at[p, 3], at_above)
+        push(d, level, p, False, at_above)
 
     def to_diag(p):
-        push(d, z, p, True, diag_send.at[p, 0], at_diag, True)
-
-    def pass_across(p, at, peer):
-        push(dd, z, p, True, diag_send.at[p, at], peer)
+        push(d, z, p, True, at_diag, True)
+
+    def pass_across(p, peer):
+        push(dd, z, p, True, peer)
 
     def to_pair(dp, level, p, bank, own=False):
         s = slot(dp, level, c)
@@ -335,9 +328,13 @@
         def go(f):
             dst = piece(s, p, f)
             src = tok_hbm.at[pl.ds(0, TILE)] if own and p == 0 else dst
-            remote(src, dst, flat_send.at[PAIR, p], pair_recv.at[p, bank], at_pair).start()
+            remote(src, dst, kind(p, f), pair_recv.at[p, bank], at_pair).start()
 
         either(True if p == 0 else hot, go)
+
+    def to_other(dp, level, p, peer):
+        part = piece(slot(dp, level, c), p, True)
+        remote(part, part, kind(p, True), pair_recv.at[p, DD], peer).start()
 
     def arrived(dp, level, p, full):
         s = slot(dp, level, c)
@@ -345,17 +342,19 @@
         def go(f):
             dst = piece(s, p, f)
             at = recv_sem.at[p, dp * levels + level]
-            remote(dst, dst, flat_send.at[X, p], at, at_x).wait_recv()
+            remote(dst, dst, send_sem.at[0], at, at_x).wait_recv()
 
         either(True if p == 0 else full, go)
 
-    pl.semaphore_wait(
-        barrier, 1 + d % 2 + d // 2 + jnp.minimum(z, 1) + z // (levels - 1) + upper_half * (d // 2)
-    )
+    lower_peers = (
+        c + d % 2 + d // 2 + jnp.minimum(z, 1) + z // (levels - 1) + upper_half * (d // 2)
+    )
+    pl.when(lower_peers > 0)(lambda: pl.semaphore_wait(barrier, lower_peers))
 
     def tell(way, peer):
         pl.semaphore_signal(ready.at[way], inc=1, device_id=peer, device_id_type=MESH)
 
+    pl.when(c == 1)(lambda: tell(5, at_pair))
     pl.when(low_x)(lambda: tell(0, at_x))
     pl.when(low_y)(lambda: tell(1, at_y))
     pl.when(low_z)(lambda: tell(3, at_below))
@@ -370,7 +369,6 @@
         pl.when(low_x)(lambda: to_x(d, z, p, True))
         pl.when(low_y)(lambda: to_y(d, z, p, True))
         pl.when(low_d)(lambda: to_diag(p))
-        to_pair(d, z, p, OWN, True)
 
     to_lower(0)
 
@@ -409,6 +407,9 @@
         slab[me, spill_at + j] = jnp.concatenate([lo, hi], axis=0).astype(bf16)
 
     to_lower(1)
+    pl.when(c == 0)(lambda: pl.semaphore_wait(ready.at[5], 1))
+    for p in range(2):
+        to_pair(d, z, p, OWN, True)
 
     def to_upper(way, up, act):
         @pl.when(up)
@@ -437,7 +438,7 @@
         def visit(level, side):
             arrived(d, level, p, True if side > 0 else hot)
             if dist == 1 and side > 0:
-                pl.when(low_z)(lambda: pass_down(level, p, 2))
+                pl.when(low_z)(lambda: pass_down(level, p))
             elif dist == 1:
                 pl.when(up_z)(lambda: pass_up(level, p))
             to_x(d, level, p)
@@ -457,10 +458,16 @@
             arrived(dx, level, p, full)
             turn = jnp.logical_and((p + c) % 2 == 0, keep)
             pl.when(turn)(lambda: to_y(dx, level, p))
+            if dist in (1, 2) and side > 0:
+                both = jnp.logical_and(turn, z == dist - 1)
+                pl.when(both)(lambda: to_other(dx, level, p, (dy, z * 2 + pc)))
             to_pair(dx, level, p, bank)
             arrived(dy, level, p, full)
             turn = jnp.logical_and((p + c) % 2 == 1, keep)
             pl.when(turn)(lambda: to_x(dy, level, p))
+            if dist in (1, 2) and side > 0:
+                both = jnp.logical_and(turn, z == dist - 1)
+                pl.when(both)(lambda: to_other(dy, level, p, (dx, z * 2 + pc)))
             to_pair(dy, level, p, bank)
 
         at_distance(dist, visit)
@@ -471,10 +478,13 @@
         def visit(level, side):
             arrived(dd, level, p, full)
             if dist == 0:
-                pl.when(last_z)(lambda: pass_across(p, 1, at_bottom))
-                pl.when(z == 2)(lambda: pass_across(p, 1, at_bottom))
-                pl.when(first_z)(lambda: pass_across(p, 1, at_above))
-            to_pair(dd, level, p, DD)
+                pl.when(last_z)(lambda: pass_across(p, at_bottom))
+                pl.when(z == 2)(lambda: pass_across(p, at_bottom))
+                pl.when(first_z)(lambda: pass_across(p, at_above))
+            if dist in (1, 2) and side > 0:
+                pl.when(z != dist - 1)(lambda: to_pair(dd, level, p, DD))
+            else:
+                to_pair(dd, level, p, DD)
 
         at_distance(dist, visit)
 
@@ -483,7 +493,7 @@
         remote(
             all_tok.at[region],
             all_tok.at[region],
-            flat_send.at[PAIR, 0],
+            send_sem.at[0],
             pair_recv.at[0, bank],
             at_pair,
         ).wait_recv()
@@ -491,7 +501,7 @@
         def go(f):
             part = slab.at[region] if f else slab.at[region, pl.ds(0, spill_at)]
             remote(
-                part, part, flat_send.at[PAIR, 1], pair_recv.at[1, bank], at_pair
+                part, part, send_sem.at[1], pair_recv.at[1, bank], at_pair
             ).wait_recv()
 
         either(hot, go)
@@ -577,6 +587,7 @@
     main_rows = experts * TILE
     group_rows = main_rows + levels * 8
     early = (all_t, all_og, all_h, all_gg, all_ug)
+    mid = (mid_t, mid_og, mid_h, mid_gg, mid_ug)
     late = (late_t, late_og, late_h, late_gg, late_ug)
 
     for p in range(2):
@@ -644,18 +655,18 @@
                 row_out[c, level, blocks:].astype(f32) + pair_in[level, blocks:].astype(f32)
             ).astype(bf16)
 
-    def z_copy(level, sender, send, peer, f):
+    def z_copy(level, sender, peer, f):
         src, dst = row_sum.at[level], z_in.at[sender]
         if not f:
             part = pl.ds(0, blocks)
             src, dst = row_sum.at[level, part], z_in.at[sender, part]
-        return remote(src, dst, z_send.at[send], z_recv.at[sender], peer)
+        return remote(src, dst, row_sem.at[0], z_recv.at[sender], peer)
 
     for level in range(levels):
 
         @pl.when(z != level)
         def _():
-            either(hot, lambda f: z_copy(level, z, level, (d, level * 2 + c), f).start())
+            either(hot, lambda f: z_copy(level, z, (d, level * 2 + c), f).start())
 
     @pl.when(low_z)
     def _():
@@ -679,21 +690,25 @@
                 for p in range(2):
                     across(dist, p)
 
-    across_when(first_z, 3, 2)
-    across_when(low_z, 1)
-    across_when(last_z, 2, 3)
     share = features // 4
     cols = pl.ds(pl.multiple_of(d * share, LANES), share)
     t_cols = all_t[:, cols]
     acc_gate[...] = lax.dot_general(t_cols, all_gg[...], TN, preferred_element_type=f32)
     acc_up[...] = lax.dot_general(t_cols, all_ug[...], TN, preferred_element_type=f32)
     acc_down[...] = lax.dot_general(all_h[...], all_og[...], TN, preferred_element_type=f32)
+    across_when(first_z, 3, 2)
+    across_when(low_z, 1)
+    across_when(last_z, 2, 3)
     from_pair(FAR, 0, levels)
-    group([(dx, far, 2), (dy, far, 2)], late + (0,))
+    group([(dx, far, 2), (dy, far, 2)], mid + (0,))
+    m_cols = mid_t[:, cols]
+    acc_gate[...] += lax.dot_general(m_cols, mid_gg[...], TN, preferred_element_type=f32)
+    acc_up[...] += lax.dot_general(m_cols, mid_ug[...], TN, preferred_element_type=f32)
+    acc_down[...] += lax.dot_general(mid_h[...], mid_og[...], TN, preferred_element_type=f32)
     across_when(first_z, 1)
     across_when(jnp.logical_and(low_z, up_z), 2)
     from_pair(DD, 0, levels)
-    group([(dd, 0, levels)], late + (group_rows,))
+    group([(dd, 0, levels)], late + (0,))
     late_cols[...] = late_t[:, cols]
     z_in[z] = row_sum[z]
 
@@ -701,7 +716,7 @@
 
         @pl.when(z != level)
         def _():
-            z_copy(level, level, level, at_pair, level < hot_levels).wait_recv()
+            z_copy(level, level, at_pair, level < hot_levels).wait_recv()
 
     total = z_in[0, :blocks].astype(f32)
     spilled = z_in[0, blocks:].astype(f32)
@@ -720,52 +735,30 @@
                 [jnp.where(kept_row, rows, 0.0), blank], axis=0
             ).astype(bf16)
 
-    def sent(send, p, count, f, first=0):
-        region = pl.ds(first, count)
-        part = all_tok.at[region]
-        if p == 1:
-            part = slab.at[region] if f else slab.at[region, pl.ds(0, spill_at)]
-        remote(part, part, send, recv_sem.at[0, 0], at_x).wait_send()
-
-    for p in range(2):
-        wide = True if p == 0 else hot
-        for way in (X, Y):
-            send = flat_send.at[way, p]
-            more = (p + c) % 2 == (1 if way == X else 0)
-            less = (p + c) % 2 == (0 if way == X else 1)
-            for at, extra in ((0, 2), (1, levels - 1), (2, levels - 1)):
-                here = (z == 0, z == 1, upper)[at]
-                own = 1 if at == 2 and p == 1 else 0
-                f = not (at == 2 and p == 1)
-                pl.when(jnp.logical_and(here, less))(
-                    functools.partial(sent, send, p, levels - own, f)
-                )
-                pl.when(jnp.logical_and(here, more))(
-                    functools.partial(sent, send, p, levels - own + extra, f)
-                )
-            if p == 1:
-                pl.when(upper)(functools.partial(sent, own_send.at[way], 1, 1, True))
-        either(wide, lambda f: sent(flat_send.at[PAIR, p], p, 4 * levels, f))
-
-        pl.when(upper)(functools.partial(sent, diag_send.at[p, 0], p, 1, True))
-        pl.when(z != 1)(functools.partial(sent, diag_send.at[p, 1], p, 1, True))
-
-        pl.when(first_z)(functools.partial(sent, z_own.at[p, 0], p, 1, False))
-        pl.when(first_z)(functools.partial(sent, z_own.at[p, 1], p, 1, True))
-        pl.when(low_z)(functools.partial(sent, z_own.at[p, 0], p, 1, True))
-        pl.when(low_z)(functools.partial(sent, z_own.at[p, 2], p, 1, True))
-
-        @pl.when(jnp.logical_and(low_z, up_z))
+    def sent(sem, slots, width):
+        part = slab.at[pl.ds(0, slots), pl.ds(0, width)]
+        remote(part, part, sem, recv_sem.at[0, 0], at_x).wait_send()
+
+    wide = slab.shape[1]
+    relays = 4 * levels
+    sides = 2 * levels
+    for level, tokens_out, full_out, cold_out in (
+        (0, relays + sides + 5, relays + sides + 4, 1),
+        (1, relays + sides + 7, relays + sides + 5, 2),
+        (2, relays + sides + 9, 6, relays + sides + 3),
+        (3, relays + sides + 7, 6, relays + sides + 1),
+    ):
+
+        @pl.when(z == level)
         def _():
-            sent(z_own.at[p, 1], p, 1, False)
-            sent(z_own.at[p, 3], p, 1, False)
-
-    either(hot, lambda f: row_copy(f).wait_send())
-    for level in range(levels):
-
-        @pl.when(z != level)
-        def _():
-            either(hot, lambda f: z_copy(level, z, level, at_pair, f).wait_send())
+            if tokens_out <= slab.shape[0]:
+                sent(send_sem.at[0], tokens_out, blocks)
+            else:
+                sent(send_sem.at[0], blocks * 3, tokens_out // 3)
+            sent(send_sem.at[1], full_out, wide)
+            sent(send_sem.at[2], cold_out, spill_at)
+
+    either(hot, lambda f: sent(row_sem.at[0], 2 * levels - 1, blocks + half if f else blocks))
 
 
 def finish_kernel(
@@ -822,7 +815,7 @@
     slots = replicas * experts
     share = features // replicas
     group_rows = experts * TILE + levels * 8
-    early_rows, late_rows = 2 * group_rows, 2 * group_rows
+    early_rows, late_rows = 2 * group_rows, group_rows
     bf16, f32 = jnp.bfloat16, jnp.float32
     vmem = pl.BlockSpec(memory_space=pltpu.VMEM)
     hbm = pl.BlockSpec(memory_space=pltpu.HBM)
@@ -874,22 +867,23 @@
             pltpu.VMEM((early_rows, hidden_size), bf16),
             pltpu.VMEM((early_rows, hidden_size), bf16),
             pltpu.VMEM((late_rows, features), bf16),
+            pltpu.VMEM((late_rows, features), bf16),
+            pltpu.VMEM((late_rows, features), bf16),
+            pltpu.VMEM((late_rows, hidden_size), bf16),
+            pltpu.VMEM((late_rows, hidden_size), bf16),
+            pltpu.VMEM((late_rows, hidden_size), bf16),
             pltpu.VMEM((2, levels, blocks + half, TILE, LANES), bf16),
             pltpu.VMEM((levels, blocks + half, TILE, LANES), bf16),
             pltpu.VMEM((levels, blocks + half, TILE, LANES), bf16),
             pltpu.VMEM((levels, blocks + half, TILE, LANES), bf16),
             dma((7,)),
             dma((3,)),
-            dma((3, 2)),
-            dma((2,)),
-            dma((2, levels)),
-            dma((2, 2)),
+            dma((3,)),
             dma((2, slots // 2)),
             dma((2, 4)),
             dma((2,)),
             dma((levels,)),
-            dma((levels,)),
-            pltpu.SemaphoreType.REGULAR((5,)),
+            pltpu.SemaphoreType.REGULAR((6,)),
         ],
         compiler_params=pltpu.CompilerParams(
             collective_id=0, has_side_effects=True, vmem_limit_bytes=32 * 1024 * 1024

time: 25.4 us -> 23.9 us (0.941)
  Pallas kernels: 24.6 us -> 23.1 us
    pallas_call x1, Pallas kernels: 23 us -> 21.8 us  [dense_shards(): pl.pallas_call(functools.partial(dense_kernel, experts), out_shape=(jax.S...]
    pallas_call x1, Pallas kernels: 1.58 us -> 1.32 us  [dense_shards(): pl.pallas_call(finish_kernel, out_shape=(jax.ShapeDtypeStruct((token_coun...]
where the time goes in v4:
time: 23.9 us; the launch traced here: 23.8 us
  Pallas kernels  23.1 us (97%)
  between operations  0.64 us (3%)
    pallas_call x1, Pallas kernels, dense_shards(): pl.pallas_call(functools.partial(dense_kernel, experts), out_shape=(jax.S...  21.8 us
    pallas_call x1, Pallas kernels, dense_shards(): pl.pallas_call(finish_kernel, out_shape=(jax.ShapeDtypeStruct((token_coun...  1.32 us

profile of v4, /device:TPU:9, one launch (start us, length us, event | category | flops | bytes accessed | tf_op | source)
XLA Modules:
  0.0 23.8 jit_solution(1818278705112586327)
XLA Ops:
  0.6 21.8 %shard_map.120 = (bf16[32,1024]{1,0:T(8,128)(2,1)S(1)}, f32[256,384]{1,0:T(8,128)S(1)}, f32[256,384]{1,0:T(8,128)S(1)}, f32[384,1024]{1,0:T(8,128)S(1)}, bf16[16...) custom-call(bf16[32,1024]{1,0:T(8,128)(2,1)} %tok_hbm.1, ...), custom_call_target="tpu_custom_call" | custom-call | tf_op jit(solution)/shard_map/pallas_call | solution.py:837
  22.5 1.3 %shard_map.121 = (bf16[32,1024]{1,0:T(8,128)(2,1)}, bf16[1,256,384]{2,1,0:T(8,128)(2,1)}, bf16[1,256,384]{2,1,0:T(8,128)(2,1)}, bf16[1,384,1024]{2,1,0:T(8,128)(2,1)}) custom-call(bf16[32,1024]{1,0:T(8,128)(2,1)S(1)} %get-tuple-element.13.tg_ref, f32[256,384]{1,0:T(8,128)S(1)} %get-tuple-element.14.acc_gate, f32[256,384]{1,0:T(8,128)S(1)} %get-tuple-element.15.acc_up, ...), custom_call_target="tpu_custom_call" | custom-call | tf_op jit(solution)/shard_map/pallas_call | solution.py:892

commit v5 on v4

--- a/solution.py
+++ b/solution.py
@@ -328,13 +328,13 @@
         def go(f):
             dst = piece(s, p, f)
             src = tok_hbm.at[pl.ds(0, TILE)] if own and p == 0 else dst
-            remote(src, dst, kind(p, f), pair_recv.at[p, bank], at_pair).start()
+            remote(src, dst, kind(p, f), pair_recv.at[bank], at_pair).start()
 
         either(True if p == 0 else hot, go)
 
     def to_other(dp, level, p, peer):
         part = piece(slot(dp, level, c), p, True)
-        remote(part, part, kind(p, True), pair_recv.at[p, DD], peer).start()
+        remote(part, part, kind(p, True), pair_recv.at[DD], peer).start()
 
     def arrived(dp, level, p, full):
         s = slot(dp, level, c)
@@ -489,20 +489,10 @@
         at_distance(dist, visit)
 
     def from_pair(bank, at, count):
-        region = pl.ds(at, count)
-        remote(
-            all_tok.at[region],
-            all_tok.at[region],
-            send_sem.at[0],
-            pair_recv.at[0, bank],
-            at_pair,
-        ).wait_recv()
-
         def go(f):
-            part = slab.at[region] if f else slab.at[region, pl.ds(0, spill_at)]
-            remote(
-                part, part, send_sem.at[1], pair_recv.at[1, bank], at_pair
-            ).wait_recv()
+            tiles = blocks + (slab.shape[1] if f else spill_at)
+            part = slab.at[pl.ds(0, tiles), pl.ds(0, count)]
+            remote(part, part, send_sem.at[0], pair_recv.at[bank], at_pair).wait_recv()
 
         either(hot, go)
 
@@ -660,7 +650,7 @@
         if not f:
             part = pl.ds(0, blocks)
             src, dst = row_sum.at[level, part], z_in.at[sender, part]
-        return remote(src, dst, row_sem.at[0], z_recv.at[sender], peer)
+        return remote(src, dst, row_sem.at[0], z_recv.at[0], peer)
 
     for level in range(levels):
 
@@ -712,11 +702,13 @@
     late_cols[...] = late_t[:, cols]
     z_in[z] = row_sum[z]
 
-    for level in range(levels):
-
-        @pl.when(z != level)
-        def _():
-            z_copy(level, level, at_pair, level < hot_levels).wait_recv()
+    def returned(low, high):
+        count = (low * (blocks + half) + high * blocks) // half
+        part = slab.at[pl.ds(0, count), pl.ds(0, half)]
+        remote(part, part, send_sem.at[0], z_recv.at[0], at_pair).wait_recv()
+
+    pl.when(hot)(lambda: returned(hot_levels - 1, levels - hot_levels))
+    pl.when(upper)(lambda: returned(hot_levels, levels - hot_levels - 1))
 
     total = z_in[0, :blocks].astype(f32)
     spilled = z_in[0, blocks:].astype(f32)
@@ -880,9 +872,9 @@
             dma((3,)),
             dma((3,)),
             dma((2, slots // 2)),
-            dma((2, 4)),
+            dma((4,)),
             dma((2,)),
-            dma((levels,)),
+            dma((1,)),
             pltpu.SemaphoreType.REGULAR((6,)),
         ],
         compiler_params=pltpu.CompilerParams(

time: 23.9 us -> 23.9 us (level)
  no operation moved by 1% of the time
where the time goes in v5:
time: 23.9 us; the launch traced here: 23.7 us
  Pallas kernels  23.1 us (97%)
  between operations  0.64 us (3%)
    pallas_call x1, Pallas kernels, dense_shards(): pl.pallas_call(functools.partial(dense_kernel, experts), out_shape=(jax.S...  21.8 us
    pallas_call x1, Pallas kernels, dense_shards(): pl.pallas_call(finish_kernel, out_shape=(jax.ShapeDtypeStruct((token_coun...  1.34 us

profile of v5, /device:TPU:9, one launch (start us, length us, event | category | flops | bytes accessed | tf_op | source)
XLA Modules:
  0.0 23.7 jit_solution(17378079420767537479)
XLA Ops:
  0.6 21.8 %shard_map.120 = (bf16[32,1024]{1,0:T(8,128)(2,1)S(1)}, f32[256,384]{1,0:T(8,128)S(1)}, f32[256,384]{1,0:T(8,128)S(1)}, f32[384,1024]{1,0:T(8,128)S(1)}, bf16[16...) custom-call(bf16[32,1024]{1,0:T(8,128)(2,1)} %tok_hbm.1, ...), custom_call_target="tpu_custom_call" | custom-call | tf_op jit(solution)/shard_map/pallas_call | solution.py:829
  22.4 1.3 %shard_map.121 = (bf16[32,1024]{1,0:T(8,128)(2,1)}, bf16[1,256,384]{2,1,0:T(8,128)(2,1)}, bf16[1,256,384]{2,1,0:T(8,128)(2,1)}, bf16[1,384,1024]{2,1,0:T(8,128)(2,1)}) custom-call(bf16[32,1024]{1,0:T(8,128)(2,1)S(1)} %get-tuple-element.13.tg_ref, f32[256,384]{1,0:T(8,128)S(1)} %get-tuple-element.14.acc_gate, f32[256,384]{1,0:T(8,128)S(1)} %get-tuple-element.15.acc_up, ...), custom_call_target="tpu_custom_call" | custom-call | tf_op jit(solution)/shard_map/pallas_call | solution.py:884

commit v6 on v5

--- a/solution.py
+++ b/solution.py
@@ -365,7 +365,13 @@
 
     def to_lower(p):
         pl.when(low_z)(lambda: to_below(p))
-        pl.when(last_z)(lambda: to_bottom(p))
+        if p == 1:
+
+            @pl.when(last_z)
+            def _():
+                to_bottom(0)
+                to_bottom(1)
+
         pl.when(low_x)(lambda: to_x(d, z, p, True))
         pl.when(low_y)(lambda: to_y(d, z, p, True))
         pl.when(low_d)(lambda: to_diag(p))

time: 23.9 us -> 23.9 us (level)
  no operation moved by 1% of the time
where the time goes in v6:
time: 23.9 us; the launch traced here: 23.7 us
  Pallas kernels  23.1 us (97%)
  between operations  0.64 us (3%)
    pallas_call x1, Pallas kernels, dense_shards(): pl.pallas_call(functools.partial(dense_kernel, experts), out_shape=(jax.S...  21.8 us
    pallas_call x1, Pallas kernels, dense_shards(): pl.pallas_call(finish_kernel, out_shape=(jax.ShapeDtypeStruct((token_coun...  1.34 us

profile of v6, /device:TPU:9, one launch (start us, length us, event | category | flops | bytes accessed | tf_op | source)
XLA Modules:
  0.0 23.7 jit_solution(12793011333896763083)
XLA Ops:
  0.6 21.8 %shard_map.120 = (bf16[32,1024]{1,0:T(8,128)(2,1)S(1)}, f32[256,384]{1,0:T(8,128)S(1)}, f32[256,384]{1,0:T(8,128)S(1)}, f32[384,1024]{1,0:T(8,128)S(1)}, bf16[16...) custom-call(bf16[32,1024]{1,0:T(8,128)(2,1)} %tok_hbm.1, ...), custom_call_target="tpu_custom_call" | custom-call | tf_op jit(solution)/shard_map/pallas_call | solution.py:835
  22.4 1.3 %shard_map.121 = (bf16[32,1024]{1,0:T(8,128)(2,1)}, bf16[1,256,384]{2,1,0:T(8,128)(2,1)}, bf16[1,256,384]{2,1,0:T(8,128)(2,1)}, bf16[1,384,1024]{2,1,0:T(8,128)(2,1)}) custom-call(bf16[32,1024]{1,0:T(8,128)(2,1)S(1)} %get-tuple-element.13.tg_ref, f32[256,384]{1,0:T(8,128)S(1)} %get-tuple-element.14.acc_gate, f32[256,384]{1,0:T(8,128)S(1)} %get-tuple-element.15.acc_up, ...), custom_call_target="tpu_custom_call" | custom-call | tf_op jit(solution)/shard_map/pallas_call | solution.py:890
